TPU v7x, 128 devices: a whole 4x4x4 slice. The times are simulated.
128 devices in a mesh: mem: 16 (over z, y), dp: 8 (over x, core).
Axes of the slice: x: 4, y: 4, z: 4, core: 2. Of those that a mesh axis runs over, the one named last changes fastest.
Arguments:
- grad_out: bfloat16 [65536, 4096], P(('mem', 'dp')), may hold values from -6 to 6
- scores: float32 [65536, 2], P(('mem', 'dp')), may hold values from -4 to 4
- row_ids: int32 [65536, 2], P(('mem', 'dp')), may hold values from 0 to 16383, as said below
- proj_ids: int32 [65536, 2], P(('mem', 'dp')), may hold values from 0 to 1
- values: bfloat16 [16384, 1024], P('mem'), may hold values from -0.1875 to 0.1875
- proj_w: bfloat16 [2, 1024, 4096], P(None, None, 'mem'), may hold values from -0.09375 to 0.09375
Outputs:
- score_grads: float32 [65536, 2], P(('mem', 'dp'))
- value_grads: bfloat16 [16384, 1024], P(('mem', 'dp'))
- proj_grads: float32 [2, 1024, 4096], P(None, 'dp', 'mem')
Inputs may be any that keep to these rules, and one draw needn't show every extreme that they name: `row_ids`: row 1024 * o + r lies on index o along mem. Of the 1024 selections of one device at most 128 name rows of one index along mem; among the devices that share one index along dp, one index along mem receives exactly 128 selections from every one of them.
All inputs are finite; a program needn't handle non-finite values.
Results may differ from a plain program's by a relative error of at most 0.012.
Values may be sent and summed in bfloat16 or wider, within the bound.
A program may use at most 128 MiB of HBM per device.

v0:
```python
import jax
import jax.numpy as jnp
from jax import lax
from jax.sharding import PartitionSpec as P


def owner_ranks(owners, owner_count):
    hits = (owners[:, None] == jnp.arange(owner_count, dtype=jnp.int32)[None, :]).astype(jnp.int32)
    before = jnp.cumsum(hits, axis=0) - hits
    return jnp.sum(before * hits, axis=1)


def local(grad_out, scores, row_ids, proj_ids, values, proj_w):
    mem_size = lax.axis_size("mem")
    mem_index = lax.axis_index("mem")
    tokens_dev, per_token = scores.shape
    rows_local, value_width = values.shape
    proj_count = proj_w.shape[0]
    sel_count = tokens_dev * per_token
    capacity = 2 * sel_count // mem_size
    projected = jnp.einsum(
        "td,pvd->ptv",
        grad_out,
        lax.all_gather(proj_w, "mem", axis=2, tiled=True),
        preferred_element_type=jnp.float32,
    )
    flat_proj = proj_ids.reshape(-1)
    flat_rows = row_ids.reshape(-1)
    flat_scores = scores.reshape(-1)
    picked = jnp.zeros((sel_count, value_width), jnp.float32)
    for which in range(proj_count):
        spread = jnp.repeat(projected[which], per_token, axis=0)
        picked = picked + jnp.where((flat_proj == which)[:, None], spread, 0.0)
    contrib = (flat_scores[:, None] * picked).astype(jnp.bfloat16)
    owners = flat_rows // rows_local
    slot_index = owners * capacity + owner_ranks(owners, mem_size)
    outgoing = (
        jnp.zeros((mem_size * capacity, value_width), jnp.bfloat16).at[slot_index].set(contrib)
    )
    incoming = lax.all_to_all(outgoing, "mem", split_axis=0, concat_axis=0, tiled=True)
    all_ids = lax.all_gather(row_ids, "mem", axis=0, tiled=True).reshape(mem_size, sel_count)
    mine = all_ids // rows_local == mem_index
    rank_mine = jnp.cumsum(mine.astype(jnp.int32), axis=1) - 1
    column = jnp.where(mine, rank_mine, capacity)
    sources = jnp.broadcast_to(
        jnp.arange(mem_size, dtype=jnp.int32)[:, None], (mem_size, sel_count)
    )
    layout = jnp.full((mem_size, capacity + 1), -1, jnp.int32)
    layout = layout.at[sources, column].set(jnp.where(mine, all_ids % rows_local, -1))
    local_rows = layout[:, :capacity].reshape(-1)
    table = (local_rows[:, None] == jnp.arange(rows_local, dtype=jnp.int32)[None, :]).astype(
        jnp.bfloat16
    )
    row_terms = lax.dot_general(
        table, incoming, (((0,), (0,)), ((), ())), preferred_element_type=jnp.float32
    )
    value_grads = lax.psum_scatter(row_terms, "dp", scatter_dimension=0, tiled=True).astype(
        jnp.bfloat16
    )
    valid = local_rows >= 0
    fetched = jnp.take(values, jnp.maximum(local_rows, 0), axis=0)
    fetched = jnp.where(valid[:, None], fetched, jnp.zeros((), jnp.bfloat16))
    returned = lax.all_to_all(fetched, "mem", split_axis=0, concat_axis=0, tiled=True)
    chosen = jnp.take(returned, slot_index, axis=0)
    chosen_wide = chosen.astype(jnp.float32)
    score_grads = jnp.sum(picked * chosen_wide, axis=1).reshape(tokens_dev, per_token)
    mix_list = []
    for which in range(proj_count):
        weight = jnp.where(flat_proj == which, flat_scores, 0.0)
        weighted = (weight[:, None] * chosen_wide).reshape(tokens_dev, per_token, value_width)
        mix_list.append(jnp.sum(weighted, axis=1).astype(jnp.bfloat16))
    mixes = jnp.stack(mix_list, axis=0)
    partial_value = jnp.einsum(
        "ptv,td->pvd", mixes, grad_out, preferred_element_type=jnp.float32
    ).astype(jnp.bfloat16)
    shares = lax.psum_scatter(partial_value, "dp", scatter_dimension=1, tiled=True).astype(
        jnp.float32
    )
    proj_grads = lax.psum_scatter(shares, "mem", scatter_dimension=2, tiled=True)
    return (score_grads, value_grads, proj_grads)


def solution(mesh):
    return jax.shard_map(
        local,
        mesh=mesh,
        in_specs=(
            P(("mem", "dp"), None),
            P(("mem", "dp"), None),
            P(("mem", "dp"), None),
            P(("mem", "dp"), None),
            P("mem", None),
            P(None, None, "mem"),
        ),
        out_specs=(P(("mem", "dp"), None), P(("mem", "dp"), None), P(None, "dp", "mem")),
        check_vma=False,
    )
```

profile of v0, /device:TPU:0, one launch (start us, length us, event | category | flops | bytes accessed | tf_op | source)
XLA Modules:
  0.0 471.6 jit_solution(9827642013135228040)
XLA Ops:
  8.1 0.7 all-gather.2.cloned.1.call-update
  8.8 25.6 %all_gather.7 = s32[8192,2]{0,1:T(2,128)S(1)} all-gather(s32[512,2]{0,1:T(2,128)} %param.8), channel_id=1, replica_groups=mesh['mem'=16,'dp'=8] {'mem'}, dimensions={0}, use_global_device_ids=true | all-gather | bytes 69632 | tf_op jit(solution)/shard_map/all_gather | solution.py:41
  34.4 2.6 copy.59
  37.0 4.1 reshape.445
  41.1 4.1 reshape.443
  45.2 4.1 reshape.442
  49.4 4.5 reduce-window.16
  54.7 60.3 %scatter_custom_fusion.1 = s32[2064]{0:T(1024)S(1)} fusion(s32[16384]{0:T(1024)S(1)} %bitcast.64, s32[16384]{0:T(1024)S(1)} %bitcast.63, s32[]{:T(128)} %constant.91.clone.1), kind=kCustom, calls=%fused_computation.97 | custom fusion | bytes 8260
  115.2 9.7 %gather_fusion = bf16[2048,1024]{1,0:T(8,128)(2,1)} fusion(bf16[1024,1024]{1,0:T(8,128)(2,1)S(1)} %copy-done, s32[2048]{0:T(1024)S(1)} %bitcast_clamp_fusion), kind=kCustom, calls=%fused_computation | custom fusion | bytes 8396800 | tf_op jit(solution)/shard_map/jit(_take)/gather | solution.py:61
  124.8 3.9 select_select_fusion
  128.7 5.0 %all-to-all-start = ((bf16[16,128,1024]{2,1,0:T(8,128)(2,1)}), bf16[16,128,1024]{2,1,0:T(8,128)(2,1)}, u32[]{:S(2)}, u32[]{:S(2)}) async-start(bf16[16,128,1024]{2,1,0:T(8,128)(2,1)} %select_select_fusion), calls=%async_computation | async-start | bytes 8388608 | tf_op jit(solution)/shard_map/all_to_all | solution.py:63
  134.5 0.2 copy.53
  134.7 4.7 reduce-window.14
  140.0 0.2 reduce_sum.43
  140.5 0.6 copy-done.5
  141.1 0.3 compare_and_fusion
  141.3 0.8 broadcast_select_fusion.2
  142.2 45.0 %all-to-all-done = bf16[16,128,1024]{2,1,0:T(8,128)(2,1)} async-done(((bf16[16,128,1024]{2,1,0:T(8,128)(2,1)}), bf16[16,128,1024]{2,1,0:T(8,128)(2,1)}, u32[]{:S(2)}, u32[]{:S(2)}) %all-to-all-start) | async-done | bytes 4194336 | tf_op jit(solution)/shard_map/all_to_all | solution.py:63
  187.1 7.7 %gather_fusion.1 = bf16[1024,1024]{1,0:T(8,128)(2,1)S(1)} fusion(bf16[2048,1024]{1,0:T(8,128)(2,1)} %bitcast.9, s32[1024]{0:T(1024)S(1)} %broadcast_clamp_fusion), kind=kCustom, calls=%fused_computation.1 | custom fusion | bytes 4198400 | tf_op jit(solution)/shard_map/jit(_take)/gather | solution.py:64
  194.9 2.5 gather.15
  197.4 17.2 %fusion.1 = (bf16[512,1024]{1,0:T(8,128)(2,1)}, bf16[512,1024]{1,0:T(8,128)(2,1)S(1)}) fusion(f32[512,2]{1,0:T(8,128)} %get-tuple-element.13, bf16[512,2,1024]{2,1,0:T(2,128)(2,1)} %gather.15, pred[512,2]{1,0:T(8,128)(4,1)S(1)} %compare_and_fusion, f32[512,2]{1,0:T(8,128)} %get-tuple-element.17), kind=kLoop, calls=%fused_computation.9 | loop fusion | flops 5242880 | bytes 4203520 | tf_op jit(solution)/shard_map/reduce_sum | solution.py:71
  214.6 1.5 copy.67
  216.1 0.5 copy.69
  216.6 13.9 %convolution_convert_fusion = bf16[2,1024,4096]{2,1,0:T(8,128)(2,1)} fusion(bf16[512,4096]{1,0:T(8,128)(2,1)} %param.6, bf16[1,512,1024]{1,2,0:T(8,128)(2,1)S(1)} %bitcast.61, bf16[1,512,1024]{1,2,0:T(8,128)(2,1)S(1)} %bitcast.60), kind=kOutput, calls=%fused_computation.4 | convolution fusion | flops 8599371776 | bytes 23068672 | tf_op jit(solution)/shard_map/ptv,td->pvd/dot_general | solution.py:73
  230.7 0.6 copy-done.3
  231.4 0.2 broadcast_in_dim.103
  231.6 0.2 broadcast_in_dim.108
  231.8 13.5 %fusion.7 = f32[2,512,1024]{1,2,0:T(8,128)S(1)} fusion(bf16[2,1024,4096]{2,1,0:T(8,128)(2,1)} %all-gather.2.cloned.1.call-done, bf16[512,4096]{1,0:T(8,128)(2,1)} %param.6), kind=kOutput, calls=%fused_computation.20 | convolution fusion | flops 8589934592 | bytes 25165824 | tf_op jit(solution)/shard_map/td,pvd->ptv/dot_general | solution.py:21
  245.2 2.5 slice_bitcast_fusion.1
  247.8 1.9 copy.45
  249.7 3.4 broadcast_in_dim.105
  253.1 6.1 %broadcast_in_dim.106 = f32[1024,1024]{1,0:T(8,128)} reshape(f32[512,2,1024]{2,1,0:T(2,128)} %broadcast_in_dim.105) | data formatting | bytes 8388608 | tf_op jit(solution)/shard_map/broadcast_in_dim | solution.py:32
  259.2 2.0 copy.47
  261.2 3.4 broadcast_in_dim.110
  264.6 6.1 %broadcast_in_dim.111 = f32[1024,1024]{1,0:T(8,128)} reshape(f32[512,2,1024]{2,1,0:T(2,128)} %broadcast_in_dim.110) | data formatting | bytes 8388608 | tf_op jit(solution)/shard_map/broadcast_in_dim | solution.py:32
  270.7 10.2 %scatter_custom_fusion = bf16[2048,1024]{1,0:T(8,128)(2,1)} fusion(s32[1024]{0:T(1024)} %bitcast.69, f32[1024]{0:T(1024)S(1)} %mul.64, bf16[]{:T(256)} %constant.100.clone.1, f32[1024,1024]{1,0:T(8,128)} %broadcast_in_dim.111, f32[1024,1024]{1,0:T(8,128)} %broadcast_in_dim.106, pred[1024]{0:T(1024)(128)(4,1)S(1)} %broadcast_in_dim.108, ...), kind=kCustom, calls=%fused_computation.21 | custom fusion | flops 5242880 | bytes 12589568 | tf_op jit(solution)/shard_map/scatter | solution.py:38
  280.9 4.5 all-to-all-start.1
  285.4 0.3 reduce-scatter.4.cloned.1.call-start
  285.7 51.8 %all-to-all-done.1 = bf16[16,128,1024]{2,1,0:T(8,128)(2,1)} async-done(((bf16[16,128,1024]{2,1,0:T(8,128)(2,1)}), bf16[16,128,1024]{2,1,0:T(8,128)(2,1)}, u32[]{:S(2)}, u32[]{:S(2)}) %all-to-all-start.1) | async-done | bytes 4194336 | tf_op jit(solution)/shard_map/all_to_all | solution.py:40
  337.5 8.8 %fusion = f32[1024,1024]{1,0:T(8,128)} fusion(bf16[2048,1024]{1,0:T(8,128)(2,1)} %bitcast.14, s32[2048]{0:T(1024)S(1)} %slice_bitcast_fusion.2), kind=kOutput, calls=%fused_computation.6 | convolution fusion | flops 4297064448 | bytes 8396800 | tf_op jit(solution)/shard_map/dot_general | solution.py:54
  346.4 4.0 convert_element_type.73
  350.5 0.2 broadcast_in_dim.112
  350.7 5.4 %multiply_reduce_fusion = f32[1024]{0:T(1024)S(1)} fusion(bf16[1024,1024]{1,0:T(8,128)(2,1)} %copy-done.2, pred[1024]{0:T(1024)(128)(4,1)S(1)} %broadcast_in_dim.112, f32[1024,1024]{1,0:T(8,128)} %broadcast_in_dim.111, pred[1024]{0:T(1024)(128)(4,1)S(1)} %broadcast_in_dim.108, f32[1024,1024]{1,0:T(8,128)} %broadcast_in_dim.106, ...), kind=kLoop, calls=%fused_computation.16 | loop fusion | flops 7339008 | bytes 10492928 | tf_op jit(solution)/shard_map/reduce_sum | solution.py:66
  356.1 0.2 reduce_sum.46
  356.3 0.7 copy.70
  357.0 25.3 %reduce-scatter.4.cloned.1.call-done = f32[128,1024]{1,0:T(8,128)} async-done(((f32[1024,1024]{1,0:T(8,128)}), f32[128,1024]{1,0:T(8,128)}) %reduce-scatter.4.cloned.1.call-update) | async-done | bytes 524304 | tf_op jit(solution)/shard_map/reduce_scatter | solution.py:57
  382.3 1.8 convert_element_type.66
  384.1 79.5 %reduce-scatter.8.cloned.1.call-done = f32[2,128,256]{2,1,0:T(8,128)} async-done(((f32[2,128,4096]{2,1,0:T(8,128)}), f32[2,128,256]{2,1,0:T(8,128)}) %reduce-scatter.8.cloned.1.call-update) | async-done | bytes 262160 | tf_op jit(solution)/shard_map/reduce_scatter | solution.py:79
  (66 shorter events, 2.8 us)
Async XLA Ops:
  8.0 107.2 %copy-start = (bf16[1024,1024]{1,0:T(8,128)(2,1)S(1)}, bf16[1024,1024]{1,0:T(8,128)(2,1)}, u32[]{:S(2)}) copy-start(bf16[1024,1024]{1,0:T(8,128)(2,1)} %param.10) | copy-start | bytes 6291460
  8.0 223.7 %all-gather.2.cloned.1.call-start = ((), (), s32[]{:S(2)}) async-start(), calls=%async_computation.5 | async-start | bytes 17825792 | tf_op jit(solution)/shard_map/all_gather | solution.py:24
  41.1 13.4 %copy-start.9 = (s32[2]{0:T(128)S(1)}, s32[2]{0:T(128)}, u32[]{:S(2)}) copy-start(s32[2]{0:T(128)} %constant.101) | copy-start | bytes 28
  41.1 13.4 %copy-start.8 = (s32[2]{0:T(128)S(1)}, s32[2]{0:T(128)}, u32[]{:S(2)}) copy-start(s32[2]{0:T(128)} %constant.104) | copy-start | bytes 28
  128.7 5.1 %copy-start.4 = (s32[512,2]{0,1:T(2,128)S(1)}, s32[512,2]{0,1:T(2,128)}, u32[]{:S(2)}) copy-start(s32[512,2]{0,1:T(2,128)} %param.8) | copy-start | bytes 12292
  128.7 11.0 %copy-start.6 = (f32[512,2]{0,1:T(2,128)S(1)}, f32[512,2]{0,1:T(2,128)}, u32[]{:S(2)}) copy-start(f32[512,2]{0,1:T(2,128)} %param.7) | copy-start | bytes 12292
  128.7 11.5 %copy-start.7 = (s32[512,2]{0,1:T(2,128)S(1)}, s32[512,2]{0,1:T(2,128)}, u32[]{:S(2)}) copy-start(s32[512,2]{0,1:T(2,128)} %param.9) | copy-start | bytes 12292
  128.7 58.4 %all-to-all-start = ((bf16[16,128,1024]{2,1,0:T(8,128)(2,1)}), bf16[16,128,1024]{2,1,0:T(8,128)(2,1)}, u32[]{:S(2)}, u32[]{:S(2)}) async-start(bf16[16,128,1024]{2,1,0:T(8,128)(2,1)} %select_select_fusion), calls=%async_computation | async-start | bytes 8388608 | tf_op jit(solution)/shard_map/all_to_all | solution.py:63
  133.8 212.7 %reduce-scatter.6.cloned.1.call-start = ((), (), s32[]{:S(2)}) async-start(), calls=%async_computation.7 | async-start | bytes 18874368 | tf_op jit(solution)/shard_map/reduce_scatter | solution.py:76
  140.5 0.6 copy-start.5
  194.9 19.7 %copy-start.2 = (bf16[1024,1024]{1,0:T(8,128)(2,1)}, bf16[1024,1024]{1,0:T(8,128)(2,1)S(1)}, u32[]{:S(2)}) copy-start(bf16[1024,1024]{1,0:T(8,128)(2,1)S(1)} %gather_fusion.1) | copy-start | bytes 6291460
  230.5 0.8 copy-start.3
  280.9 56.7 %all-to-all-start.1 = ((bf16[16,128,1024]{2,1,0:T(8,128)(2,1)}), bf16[16,128,1024]{2,1,0:T(8,128)(2,1)}, u32[]{:S(2)}, u32[]{:S(2)}) async-start(bf16[16,128,1024]{2,1,0:T(8,128)(2,1)} %bitcast.58), calls=%async_computation.1 | async-start | bytes 8388608 | tf_op jit(solution)/shard_map/all_to_all | solution.py:40
  285.4 96.9 %reduce-scatter.4.cloned.1.call-start = ((), (), s32[]{:S(2)}) async-start(), calls=%async_computation.6 | async-start | bytes 4718592 | tf_op jit(solution)/shard_map/reduce_scatter | solution.py:57
  346.4 117.2 %reduce-scatter.8.cloned.1.call-start = ((), (), s32[]{:S(2)}) async-start(), calls=%async_computation.8 | async-start | bytes 4456448 | tf_op jit(solution)/shard_map/reduce_scatter | solution.py:79
  350.5 113.1 %copy-start.1 = (bf16[1024,1024]{1,0:T(8,128)(2,1)S(1)}, bf16[1024,1024]{1,0:T(8,128)(2,1)}, u32[]{:S(2)}) copy-start(bf16[1024,1024]{1,0:T(8,128)(2,1)} %param.10) | copy-start | bytes 6291460
Sparse Core Ops, SparseCore 0:
  10.9 140.5 all-gather.1
Sparse Core Ops, SparseCore 1:
  230.6 88.4 reduce-scatter.5
  346.4 35.8 reduce-scatter.3
  386.1 77.4 reduce-scatter.7
where the time goes:
time: 478 us; the launch traced here: 472 us
  waiting for transfers between devices  202 us (42%)
  local copies, waits for them, and re-layouts  128 us (27%)
  other arithmetic  53.4 us (11%)
  matrix products  36.2 us (8%)
  blocking collectives  25.6 us (5%)
  between operations  16.5 us (3%)
  starting transfers between devices  10 us (2%)
    reduce_scatter x1, waiting for transfers between devices, local(): lax.psum_scatter(shares, 'mem', scatter_dimension=2, tiled=True)  79.5 us
    unnamed x27, local copies, waits for them, and re-layouts  62.8 us
    all_to_all x1, waiting for transfers between devices, local(): lax.all_to_all(outgoing, 'mem', split_axis=0, concat_axis=0, tiled=True)  51.8 us
    all_to_all x1, waiting for transfers between devices, local(): lax.all_to_all(fetched, 'mem', split_axis=0, concat_axis=0, tiled=True)  45 us
    all_gather x1, blocking collectives, local(): lax.all_gather(row_ids, 'mem', axis=0, tiled=True)  25.6 us
    reduce_scatter x1, waiting for transfers between devices, local(): lax.psum_scatter(row_terms, 'dp', scatter_dimension=0, tiled=True)  25.3 us
    broadcast_in_dim x4, local copies, waits for them, and re-layouts, local(): spread = jnp.repeat(projected[which], per_token, axis=0)  19 us
    reduce_sum x1, other arithmetic, local(): mix_list.append(jnp.sum(weighted, axis=1).astype(jnp.bfloat16))  17.2 us
  transfers between devices with their start and end apart: 6, of which 4 were waited for; matrix products, arithmetic and copies ran while one was open for 46% of the time, Pallas kernels for 0%

commit v1 on v0

v1 whole, which is shorter than its diff:
```python
import jax
import jax.numpy as jnp
from jax import lax
from jax.experimental import pallas as pl
from jax.experimental.pallas import tpu as pltpu
from jax.sharding import PartitionSpec as P

F32 = jnp.float32
BF16 = jnp.bfloat16
I32 = jnp.int32
MESH = pl.DeviceIdType.MESH
ORDER = (4, 1, 12, 3, 8, 2, 5, 15, 7, 13, 9, 6, 11, 14, 10)
PACKS = tuple(sum(label * 16**place for place, label in enumerate(ORDER[at : at + 5])) for at in (0, 5, 10))


def in_order(body):
    for pack in PACKS:

        def step(_, carry):
            body(carry % 16)
            return carry // 16

        lax.fori_loop(0, 5, step, jnp.int32(pack))


def loop(count, body, start=0):
    def step(index, carry):
        body(index)
        return carry

    lax.fori_loop(start, count, step, jnp.int32(0))


def nn(a, b):
    return lax.dot_general(a, b, (((1,), (0,)), ((), ())), preferred_element_type=F32)


def nt(a, b):
    return lax.dot_general(a, b, (((1,), (1,)), ((), ())), preferred_element_type=F32)


def hot(condition):
    return jnp.where(condition, F32(1), F32(0)).astype(BF16)


def kernel(
    grad_hbm, scores_ref, rows_ref, proj_ref, values_hbm, w_hbm,
    sg_out, vg_out, pg_out,
    gbuf, wg, vh, outbox, chosen_in, contrib_in, chosen, pb, ra, rb, rl, rr, fr,
    vgs, vgr, vgp_s, vgp_r, metas, slotr, slotc, reqs, reqr, sgs, sgr,
    lsem, core_s, core_r, req_s, req_r, val_s, val_r, wq_s, wq_r, w1_s, w1_r, w2_s, w2_r, wx_s, wx_r,
    p2_s, p2_r, p1_s, p1_r, p3_s, p3_r, con_s, con_r, fin_s, fin_r, vx_s, vx_r,
):
    m = lax.axis_index("mem")
    d = lax.axis_index("dp")
    z, y = m // 4, m % 4
    x, c = d // 2, d % 2
    partner = (m, x * 2 + (1 - c))

    def peer_mem(label):
        return ((z + label // 4) % 4) * 4 + (y + label % 4) % 4

    def peer(label):
        return (peer_mem(label), d)

    def xpeer(step):
        return (m, ((x + step) % 4) * 2 + c)

    def remote(src, dst, send, recv, device):
        return pltpu.make_async_remote_copy(
            src_ref=src, dst_ref=dst, send_sem=send, recv_sem=recv, device_id=device, device_id_type=MESH
        )

    local_copies = [pltpu.make_async_copy(grad_hbm, gbuf.at[0], lsem.at[0])]
    for j in range(4):
        block = (x + j) % 4
        local_copies.append(
            pltpu.make_async_copy(
                values_hbm.at[:, pl.ds(pl.multiple_of(block * 256 + c * 128, 128), 128)],
                vh.at[:, pl.ds(j * 128, 128)],
                lsem.at[1 + j],
            )
        )
    w_copies = []
    for p in range(2):
        for j in range(4):
            w_copies.append(
                pltpu.make_async_copy(
                    w_hbm.at[p, (x + j) % 4, c], wg.at[0, p, pl.ds(j * 128, 128)], lsem.at[5 + p * 4 + j]
                )
            )
    for copy in w_copies + local_copies:
        copy.start()

    barrier = pltpu.get_barrier_semaphore()
    for label in range(1, 16):
        pl.semaphore_signal(barrier, inc=1, device_id=peer(label), device_id_type=MESH)
    for step in range(1, 4):
        pl.semaphore_signal(barrier, inc=1, device_id=xpeer(step), device_id_type=MESH)
    pl.semaphore_signal(barrier, inc=1, device_id=partner, device_id_type=MESH)

    lane = lax.broadcasted_iota(I32, (512, 128), 1)
    meta = jnp.zeros((512, 128), F32)
    for at, ref in enumerate((rows_ref, proj_ref, scores_ref)):
        for s in range(2):
            meta = jnp.where(lane == 2 * at + s, ref[:, s : s + 1].astype(F32), meta)
    metas[0] = meta
    pl.semaphore_wait(barrier, 19)

    meta_copy = remote(metas.at[0], metas.at[1], core_s.at[0], core_r.at[0], partner)
    meta_copy.start()
    for copy in w_copies:
        copy.wait()

    def quarter(label):
        here = wg.at[0, 1, pl.ds(0, 128)]
        return remote(here, wg.at[label, 1, pl.ds(0, 128)], wq_s.at[label], wq_r.at[label], peer(label))

    def stage_one(half, step):
        label = step * 4 if half == 0 else step
        rows = pl.ds(half * 256, 256)
        return remote(
            wg.at[0, 0, rows], wg.at[label, 0, rows], w1_s.at[half, step], w1_r.at[half, step], peer(label)
        )

    def stage_two(half, held, step):
        source, move = (held * 4, step) if half == 0 else (held, step * 4)
        rows = pl.ds(half * 256, 256)
        return remote(
            wg.at[source, 0, rows],
            wg.at[source + move, 0, rows],
            w2_s.at[half, source + move],
            w2_r.at[half, source + move],
            peer(move),
        )

    def along_x(label, step):
        return remote(
            wg.at[label, 1, pl.ds(0, 128)],
            wg.at[label, 1, pl.ds((4 - step) * 128, 128)],
            wx_s.at[label, step],
            wx_r.at[label, 4 - step],
            xpeer(step),
        )

    in_order(lambda label: quarter(label).start())
    for step in (1, 3, 2):
        for half in range(2):
            stage_one(half, step).start()
    grad_copy = remote(grad_hbm, gbuf.at[1], core_s.at[1], core_r.at[1], partner)
    grad_copy.start()

    reqs[...] = jnp.zeros_like(reqs)
    for k in range(2):
        if k == 1:
            meta_copy.wait_recv()
        flat = jnp.transpose(metas[k])
        row = jnp.concatenate([flat[0:1, :], flat[1:2, :]], axis=1).astype(I32)
        owner = row >> 10
        label = ((((owner >> 2) - z) & 3) << 2) | (((owner & 3) - y) & 3)
        hit = label == lax.broadcasted_iota(I32, (16, 1024), 0)
        hits = hot(hit)
        before = []
        for part in range(4):
            upper = lax.broadcasted_iota(I32, (1024, 256), 0) < lax.broadcasted_iota(I32, (1024, 256), 1) + part * 256
            before.append(nn(hits, hot(upper)))
        before = jnp.concatenate(before, axis=1)
        rank = jnp.sum(jnp.where(hit, before, F32(0)), axis=0, keepdims=True)
        slot = label.astype(F32) * 128 + rank
        slotr[k] = jnp.broadcast_to(slot, (8, 1024)).astype(I32)
        slotc[k] = jnp.transpose(jnp.broadcast_to(slot, (128, 1024)))
        rank_column = jnp.transpose(jnp.broadcast_to(rank, (128, 1024)))
        places = hot(rank_column == lax.broadcasted_iota(I32, (1024, 128), 1).astype(F32))
        number = (row & 1023) + 1
        upper_digit = jnp.where(hit, (number >> 5).astype(F32), F32(0)).astype(BF16)
        lower_digit = jnp.where(hit, (number & 31).astype(F32), F32(0)).astype(BF16)
        asked = nn(upper_digit, places) * 32 + nn(lower_digit, places) - 1
        for label_at in range(16):
            reqs[label_at, k : k + 1, :] = asked[label_at : label_at + 1, :]

    def request(label):
        return remote(reqs.at[label], reqr.at[label], req_s.at[label], req_r.at[label], peer(label))

    in_order(lambda label: request(label).start())
    reqr[0] = reqs[0]
    for copy in local_copies:
        copy.wait()

    def value_copy(label):
        back = ((z + 4 - label // 4) % 4) * 4 + (y + 4 - label % 4) % 4
        return remote(
            outbox.at[:, label], chosen_in.at[:, label], val_s.at[label], val_r.at[label], (back, d)
        )

    def look_up(label, target):
        parts = []
        for k in range(2):
            column = jnp.transpose(jnp.broadcast_to(reqr[label, k : k + 1, :], (128, 128)))
            base = lax.broadcasted_iota(I32, (128, 128), 1).astype(F32)
            parts.append(jnp.concatenate([hot(column == base + 128 * part) for part in range(8)], axis=1))
        found = nn(jnp.concatenate(parts, axis=0), vh[...]).astype(BF16)
        target[0, label] = found[:128]
        target[1, label] = found[128:]

    def serve(label):
        request(label).wait_recv()
        look_up(label, outbox)
        value_copy(label).start()

    in_order(serve)
    look_up(0, chosen_in)

    for held in range(4):
        if held:
            for half in range(2):
                stage_one(half, held).wait_recv()
        for step in (1, 3, 2):
            for half in range(2):
                stage_two(half, held, step).start()

    def forward(label):
        quarter(label).wait_recv()
        for step in (1, 3, 2):
            along_x(label, step).start()

    in_order(forward)

    in_order(lambda label: value_copy(label).wait_recv())
    grad_copy.wait_recv()

    def choose(at):
        k, tile = at // 2, at % 2
        column = slotc[k, pl.ds(pl.multiple_of(tile * 512, 512), 512), :]
        base = lax.broadcasted_iota(I32, (512, 128), 1).astype(F32)
        table = jnp.concatenate([hot(column == base + 128 * part) for part in range(16)], axis=1)
        rows = nn(table, chosen_in[k].reshape(2048, 512))
        chosen[k, pl.ds(pl.multiple_of(tile * 512, 512), 512), :] = rows.astype(BF16)

    loop(4, choose)

    def scope_mix(mt):
        for k in range(2):

            def mix(tile):
                here = pl.ds(pl.multiple_of(tile * 128, 128), 128)
                first = chosen[k, here, :].astype(F32)
                second = chosen[k, pl.ds(pl.multiple_of(512 + tile * 128, 128), 128), :].astype(F32)
                for p in range(2):
                    w0 = jnp.where(metas[k, here, 2:3] == p, metas[k, here, 4:5], F32(0))
                    w1 = jnp.where(metas[k, here, 3:4] == p, metas[k, here, 5:6], F32(0))
                    turned = jnp.transpose(w0 * first + w1 * second).astype(BF16)
                    for j in range(4):
                        mt[
                            pl.ds(j * 256 + p * 128, 128),
                            pl.ds(pl.multiple_of(k * 512 + tile * 128, 128), 128),
                        ] = turned[j * 128 : (j + 1) * 128]

            loop(4, mix)

        for a in range(4):

            def partial(b):
                columns = pl.ds(pl.multiple_of((((z + a) % 4) * 4 + (y + b) % 4) * 256, 256), 256)
                term = nn(mt[:, :512], gbuf[0, :, columns]) + nn(mt[:, 512:], gbuf[1, :, columns])
                term = term.astype(BF16)
                for j in range(4):
                    pb[j, a * 4 + b] = term[j * 256 : (j + 1) * 256]

            loop(4, partial)
            two_away(a).start()
            if a < 2:
                to_left(a).start()
            else:
                to_right(a).start()

    def span(a):
        return pl.ds(a * 4, 4)

    def two_away(a):
        if a < 2:
            return remote(pb.at[2, span(a)], ra.at[span(a)], p2_s.at[a], p2_r.at[a], xpeer(1))
        return remote(pb.at[2, span(a)], rb.at[span(a - 2)], p2_s.at[a], p2_r.at[a], xpeer(3))

    def to_right(a):
        return remote(pb.at[1, span(a)], rl.at[span(a)], p1_s.at[a], p1_r.at[a], xpeer(1))

    def to_left(a):
        return remote(pb.at[3, span(a)], rr.at[span(a)], p3_s.at[a], p3_r.at[a], xpeer(3))

    pl.run_scoped(scope_mix, pltpu.VMEM((1024, 1024), BF16))

    def merge(a):
        two_away(a).wait_recv()
        block, arrived, shift = (1, ra, 0) if a < 2 else (3, rb, 8)

        def add(b):
            at = a * 4 + b
            pb[block, at] = (pb[block, at].astype(F32) + arrived[at - shift].astype(F32)).astype(BF16)

        loop(4, add)
        (to_right(a) if a < 2 else to_left(a)).start()

    def contrib_copy(label):
        return remote(outbox.at[:, label], contrib_in.at[:, label], con_s.at[label], con_r.at[label], peer(label))

    def score_copy():
        return remote(sgs.at[1], sgr, core_s.at[2], core_r.at[2], partner)

    def scope_pick(pr, contrib):
        def columns_of(label):
            return pl.ds(pl.multiple_of(peer_from(label) * 256, 256), 256)

        def peer_from(label):
            return ((z + 4 - label // 4) % 4) * 4 + (y + 4 - label % 4) % 4

        def project(label, p, first=False):
            for k in range(2):
                term = nt(gbuf[k, :, columns_of(label)], wg[label, p])
                here = (pl.ds(k * 512, 512), pl.ds(p * 512, 512))
                pr[here] = term if first else pr[here] + term

        for p in (1, 0):
            project(0, p, True)

        def second(label):
            for step in range(1, 4):
                along_x(label, 4 - step).wait_recv()
            project(label, 1)

        loop(16, second, 1)
        merge(0)
        merge(2)
        for held in range(1, 4):
            for half in range(2):
                stage_two(half, 0, held).wait_recv()

        def from_stage(held):
            for half in range(2):
                for step in range(1, 4):
                    stage_two(half, held, step).wait_recv()

        for held in range(1, 4):
            from_stage(held)
        loop(16, lambda label: project(label, 0), 1)
        merge(1)
        merge(3)

        in_order(lambda label: value_copy(label).wait_send())
        for k in range(2):

            def pick(tile):
                here = pl.ds(pl.multiple_of(tile * 128, 128), 128)
                wide = pr[pl.ds(pl.multiple_of(k * 512 + tile * 128, 128), 128), :]
                lanes = lax.broadcasted_iota(I32, (128, 128), 1)
                kept = jnp.zeros((128, 128), F32)
                for s in range(2):
                    rows = pl.ds(pl.multiple_of(s * 512 + tile * 128, 128), 128)
                    picked = jnp.where(metas[k, here, 2 + s : 3 + s] == 0, wide[:, :512], wide[:, 512:])
                    contrib[k, rows, :] = (metas[k, here, 4 + s : 5 + s] * picked).astype(BF16)
                    total = jnp.sum(picked * chosen[k, rows, :].astype(F32), axis=1, keepdims=True)
                    kept = jnp.where(lanes == s, total, kept)
                sgs[k, here, :] = kept

            loop(4, pick)
        score_copy().start()

        def pack(label, target):
            for k in range(2):
                places = lax.broadcasted_iota(I32, (128, 1024), 0) + label * 128
                target[k, label] = nn(hot(slotr[k, 0:1, :] == places), contrib[k]).astype(BF16)

        def send(label):
            pack(label, outbox)
            contrib_copy(label).start()

        in_order(send)
        pack(0, contrib_in)

    pl.run_scoped(scope_pick, pltpu.VMEM((1024, 1024), F32), pltpu.VMEM((2, 1024, 512), BF16))

    def final_copy(label):
        return remote(pb.at[0, label], fr.at[label], fin_s.at[label], fin_r.at[label], peer(label))

    for a in (2, 0, 3, 1):
        to_right(a).wait_recv()
        to_left(a).wait_recv()

        def finish(b):
            at = a * 4 + b
            total = pb[0, at].astype(F32) + rl[at].astype(F32) + rr[at].astype(F32)
            pb[0, at] = total.astype(BF16)

        loop(4, finish)
        for b in range(4):
            if a * 4 + b:
                final_copy(a * 4 + b).start()

    def vg_copy(step):
        return remote(vgs.at[step], vgr.at[step], vx_s.at[step], vx_r.at[step], xpeer(step))

    def vg_partner():
        return remote(vgp_s, vgp_r, core_s.at[3], core_r.at[3], partner)

    def scope_values(vg):
        def gather(label, first=False):
            parts = []
            for k in range(2):
                places = lax.broadcasted_iota(I32, (1024, 128), 0).astype(F32)
                parts.append(hot(places == reqr[label, k : k + 1, :]))
            rows = jnp.concatenate([contrib_in[0, label], contrib_in[1, label]], axis=0)
            term = nn(jnp.concatenate(parts, axis=1), rows)
            vg[...] = term if first else vg[...] + term

        gather(0, True)

        def arrive(label):
            contrib_copy(label).wait_recv()
            gather(label)

        in_order(arrive)
        for step in (1, 3, 2):
            rows = pl.ds(pl.multiple_of(((x + step) % 4) * 256, 256), 256)
            for j in range(4):
                vgs[step, :, pl.ds(j * 128, 128)] = vg[rows, pl.ds((step + j) % 4 * 128, 128)].astype(BF16)
            vg_copy(step).start()
        own = vg[pl.ds(pl.multiple_of(x * 256, 256), 256), :]
        for step in (1, 3, 2):
            vg_copy(step).wait_recv()
            own = own + vgr[step].astype(F32)
        vg[:256, :] = own
        vgp_s[...] = vg[pl.ds(pl.multiple_of((1 - c) * 128, 128), 128), :].astype(BF16)
        vg_partner().start()
        mine = vg[pl.ds(pl.multiple_of(c * 128, 128), 128), :].astype(BF16)
        for j in range(4):
            at = pl.multiple_of(((x + j) % 4) * 256 + c * 128, 128)
            vg_out[:, pl.ds(at, 128)] = mine[:, j * 128 : (j + 1) * 128]

    pl.run_scoped(scope_values, pltpu.VMEM((1024, 512), F32))

    in_order(lambda label: final_copy(label).wait_recv())
    for p in range(2):
        rows = pl.ds(p * 128, 128)
        total = pb[0, 0, rows, :].astype(F32)
        for label in range(1, 16):
            total = total + fr[label, rows, :].astype(F32)
        pg_out[p] = total

    score_copy().wait_recv()
    sg_out[...] = sgs[0, :, 0:2] + sgr[:, 0:2]

    vg_partner().wait_recv()
    other = vgp_r[...]
    for j in range(4):
        at = pl.multiple_of(((x + j) % 4) * 256 + (1 - c) * 128, 128)
        vg_out[:, pl.ds(at, 128)] = other[:, j * 128 : (j + 1) * 128]

    meta_copy.wait_send()
    grad_copy.wait_send()
    score_copy().wait_send()
    vg_partner().wait_send()

    def sent(label):
        quarter(label).wait_send()
        request(label).wait_send()
        contrib_copy(label).wait_send()
        final_copy(label).wait_send()
        for step in range(1, 4):
            along_x(label, step).wait_send()

    loop(16, sent, 1)
    for step in range(1, 4):
        vg_copy(step).wait_send()
        for half in range(2):
            stage_one(half, step).wait_send()
            for held in range(4):
                stage_two(half, held, step).wait_send()
    for a in range(4):
        two_away(a).wait_send()
        to_right(a).wait_send()
        to_left(a).wait_send()


def local(grad_out, scores, row_ids, proj_ids, values, proj_w):
    vmem = pl.BlockSpec(memory_space=pltpu.VMEM)
    anywhere = pl.BlockSpec(memory_space=pl.ANY)
    dma = pltpu.SemaphoreType.DMA
    return pl.pallas_call(
        kernel,
        out_shape=(
            jax.ShapeDtypeStruct((512, 2), F32),
            jax.ShapeDtypeStruct((128, 1024), BF16),
            jax.ShapeDtypeStruct((2, 128, 256), F32),
        ),
        in_specs=[anywhere, vmem, vmem, vmem, anywhere, anywhere],
        out_specs=(vmem, vmem, vmem),
        scratch_shapes=[
            pltpu.VMEM((2, 512, 4096), BF16),
            pltpu.VMEM((16, 2, 512, 256), BF16),
            pltpu.VMEM((1024, 512), BF16),
            pltpu.VMEM((2, 16, 128, 512), BF16),
            pltpu.VMEM((2, 16, 128, 512), BF16),
            pltpu.VMEM((2, 16, 128, 512), BF16),
            pltpu.VMEM((2, 1024, 512), BF16),
            pltpu.VMEM((4, 16, 256, 256), BF16),
            pltpu.VMEM((8, 256, 256), BF16),
            pltpu.VMEM((8, 256, 256), BF16),
            pltpu.VMEM((16, 256, 256), BF16),
            pltpu.VMEM((16, 256, 256), BF16),
            pltpu.VMEM((16, 256, 256), BF16),
            pltpu.VMEM((4, 256, 512), BF16),
            pltpu.VMEM((4, 256, 512), BF16),
            pltpu.VMEM((128, 512), BF16),
            pltpu.VMEM((128, 512), BF16),
            pltpu.VMEM((2, 512, 128), F32),
            pltpu.VMEM((2, 8, 1024), I32),
            pltpu.VMEM((2, 1024, 128), F32),
            pltpu.VMEM((16, 8, 128), F32),
            pltpu.VMEM((16, 8, 128), F32),
            pltpu.VMEM((2, 512, 128), F32),
            pltpu.VMEM((512, 128), F32),
            dma((13,)),
            dma((4,)),
            dma((4,)),
            dma((16,)),
            dma((16,)),
            dma((16,)),
            dma((16,)),
            dma((16,)),
            dma((16,)),
            dma((2, 4)),
            dma((2, 4)),
            dma((2, 16)),
            dma((2, 16)),
            dma((16, 4)),
            dma((16, 4)),
            dma((4,)),
            dma((4,)),
            dma((4,)),
            dma((4,)),
            dma((4,)),
            dma((4,)),
            dma((16,)),
            dma((16,)),
            dma((16,)),
            dma((16,)),
            dma((4,)),
            dma((4,)),
        ],
        compiler_params=pltpu.CompilerParams(
            collective_id=0, has_side_effects=True, vmem_limit_bytes=67043328
        ),
        name="step",
    )(grad_out, scores, row_ids, proj_ids, values, proj_w.reshape(2, 4, 2, 128, 256))


def solution(mesh):
    return jax.shard_map(
        local,
        mesh=mesh,
        in_specs=(
            P(("mem", "dp"), None),
            P(("mem", "dp"), None),
            P(("mem", "dp"), None),
            P(("mem", "dp"), None),
            P("mem", None),
            P(None, None, "mem"),
        ),
        out_specs=(P(("mem", "dp"), None), P(("mem", "dp"), None), P(None, "dp", "mem")),
        check_vma=False,
    )
```

time: 478 us -> 240 us (0.50)
  Pallas kernels: 0 us -> 226 us
  waiting for transfers between devices: 202 us -> 0 us
  local copies, waits for them, and re-layouts: 128 us -> 9.6 us
  other arithmetic: 53.4 us -> 0 us
  matrix products: 36.2 us -> 0 us
  blocking collectives: 25.6 us -> 0 us
  between operations: 16.5 us -> 0.64 us
  starting transfers between devices: 10 us -> 0 us
    pallas_call x0 -> x1, Pallas kernels: none -> 226 us  [local(): pl.pallas_call(kernel, out_shape=(jax.ShapeDtypeStruct((512, 2), F32), ja...]
    reduce_scatter x3 -> x0, waiting for transfers between devices: 105 us -> none  [the longest x1 79.5 us: local(): lax.psum_scatter(shares, 'mem', scatter_dimension=2, tiled=True)]
    all_to_all x2 -> x0, waiting for transfers between devices: 96.8 us -> none  [the longest x1 51.8 us: local(): lax.all_to_all(outgoing, 'mem', split_axis=0, concat_axis=0, tiled=True)]
    unnamed x27 -> x5, local copies, waits for them, and re-layouts: 62.8 us -> 7.95 us
    dot_general x3 -> x0, matrix products: 36.2 us -> none  [the longest x1 13.9 us: local(): jnp.einsum('ptv,td->pvd', mixes, grad_out, preferred_element_type=jnp.flo...]
    all_gather x1 -> x0, blocking collectives: 25.6 us -> none  [local(): lax.all_gather(row_ids, 'mem', axis=0, tiled=True)]
    reduce_sum x3 -> x0, other arithmetic: 22.6 us -> none  [the longest x1 17.2 us: local(): mix_list.append(jnp.sum(weighted, axis=1).astype(jnp.bfloat16))]
    gather x3 -> x0, local copies, waits for them, and re-layouts: 19.9 us -> none  [the longest x2 10.2 us: local(): chosen = jnp.take(returned, slot_index, axis=0)]
  transfers between devices with their start and end apart: 6 -> 0, of which waited for: 4 -> 0; matrix products, arithmetic and copies ran while one was open for 46% -> 0% of each run, Pallas kernels for 0% -> 0%
where the time goes in v1:
time: 240 us; the launch traced here: 237 us
  Pallas kernels  226 us (94%)
  local copies, waits for them, and re-layouts  9.6 us (4%)
    pallas_call x1, Pallas kernels, local(): pl.pallas_call(kernel, out_shape=(jax.ShapeDtypeStruct((512, 2), F32), ja...  226 us
    unnamed x5, local copies, waits for them, and re-layouts  7.95 us

profile of v1, /device:TPU:0, one launch (start us, length us, event | category | flops | bytes accessed | tf_op | source)
XLA Modules:
  0.0 236.7 jit_solution(7324027280398406809)
XLA Ops:
  0.6 1.5 copy.9.scores_ref
  2.2 1.5 copy.10.rows_ref
  3.7 1.5 copy.11.proj_ref
  5.2 226.4 %step.1 = (f32[512,2]{1,0:T(8,128)}, bf16[128,1024]{1,0:T(8,128)(2,1)}, f32[2,128,256]{2,1,0:T(8,128)}) custom-call(bf16[512,4096]{1,0:T(8,128)(2,1)} %grad_hbm.1, f32[512,2]{1,0:T(8,128)} %copy.9.scores_ref, s32[512,2]{1,0:T(8,128)} %copy.10.rows_ref, s32[512,2]{1,0:T(8,128)} %copy.11.proj_ref, bf16[1024,1024]{1,0:T(8,128)(2,1)} %values_hbm.1, ...), custom_call_target="tpu_custom_call" | custom-call | tf_op jit(solution)/shard_map/step/pallas_call | solution.py:487
  231.7 1.7 copy.12
  233.3 1.7 copy.15
  235.0 1.7 copy.16

commit v2 on v1

v2 whole, which is shorter than its diff:
```python
import jax
import jax.numpy as jnp
from jax import lax
from jax.experimental import pallas as pl
from jax.experimental.pallas import tpu as pltpu
from jax.sharding import PartitionSpec as P

F32 = jnp.float32
BF16 = jnp.bfloat16
I32 = jnp.int32
MESH = pl.DeviceIdType.MESH
ORDER = (4, 1, 12, 3, 8, 2, 5, 15, 7, 13, 9, 6, 11, 14, 10)
JORDER = (2, 3, 1, 0)
PLACE = (3, 2, 0, 1)
WROW = (0, 2, 1, 3)
PACKS = tuple(sum(label * 16**place for place, label in enumerate(ORDER[at : at + 5])) for at in (0, 5, 10))


def in_order(body, packs=PACKS):
    for pack in packs:

        def step(_, carry):
            body(carry % 16)
            return carry // 16

        lax.fori_loop(0, 5, step, jnp.int32(pack))


def loop(count, body, start=0):
    def step(index, carry):
        body(index)
        return carry

    lax.fori_loop(start, count, step, jnp.int32(0))


def nn(a, b):
    return lax.dot_general(a, b, (((1,), (0,)), ((), ())), preferred_element_type=F32)


def nt(a, b):
    return lax.dot_general(a, b, (((1,), (1,)), ((), ())), preferred_element_type=F32)


def hot(condition):
    return jnp.where(condition, F32(1), F32(0)).astype(BF16)


def kernel(
    grad_hbm, scores_ref, rows_ref, proj_ref, values_hbm, w_hbm,
    sg_out, vg_out, pg_out,
    gbuf, wg, vh, outbox, chosen_in, contrib_in, chosen, pb, ra, rb, rl, rr, f1, f2,
    vgs, vgr, vgp_s, vgp_r, metar, metas, slotr, slotc, reqs, reqr, sgs, sgr,
    lsem, core_s, core_r, req_s, req_r, val_s, val_r, w1_s, w1_r, wq_s, wq_r, wx_s, wx_r,
    p2_s, p2_r, p1_s, p1_r, p3_s, p3_r, con_s, con_r, f1_s, f1_r, f2_s, f2_r, vx_s, vx_r,
):
    m = lax.axis_index("mem")
    d = lax.axis_index("dp")
    z, y = m // 4, m % 4
    x, c = d // 2, d % 2
    partner = (m, x * 2 + (1 - c))

    def peer_mem(label):
        return ((z + label // 4) % 4) * 4 + (y + label % 4) % 4

    def peer(label):
        return (peer_mem(label), d)

    def xpeer(step):
        return (m, ((x + step) % 4) * 2 + c)

    def remote(src, dst, send, recv, device):
        return pltpu.make_async_remote_copy(
            src_ref=src, dst_ref=dst, send_sem=send, recv_sem=recv, device_id=device, device_id_type=MESH
        )

    local_copies = [pltpu.make_async_copy(grad_hbm, gbuf.at[0], lsem.at[0])]
    for q in range(4):
        block = (x + JORDER[q]) % 4
        local_copies.append(
            pltpu.make_async_copy(
                values_hbm.at[:, pl.ds(pl.multiple_of(block * 256 + c * 128, 128), 128)],
                vh.at[:, pl.ds(q * 128, 128)],
                lsem.at[1 + q],
            )
        )
    w_copies = []
    for p in range(2):
        for q in range(4):
            w_copies.append(
                pltpu.make_async_copy(
                    w_hbm.at[p, (x + JORDER[q]) % 4, c], wg.at[0, p, pl.ds(WROW[JORDER[q]] * 128, 128)], lsem.at[5 + p * 4 + q]
                )
            )
    for copy in w_copies + local_copies:
        copy.start()

    barrier = pltpu.get_barrier_semaphore()
    for label in range(1, 16):
        pl.semaphore_signal(barrier, inc=1, device_id=peer(label), device_id_type=MESH)
    for step in range(1, 4):
        pl.semaphore_signal(barrier, inc=1, device_id=xpeer(step), device_id_type=MESH)
    pl.semaphore_signal(barrier, inc=1, device_id=partner, device_id_type=MESH)

    metar[0] = jnp.concatenate(
        [rows_ref[...].astype(F32), proj_ref[...].astype(F32), scores_ref[...], jnp.zeros((2, 512), F32)], axis=0
    )
    pl.semaphore_wait(barrier, 19)

    meta_copy = remote(metar.at[0], metar.at[1], core_s.at[0], core_r.at[0], partner)
    meta_copy.start()
    for copy in w_copies:
        copy.wait()

    mine = pl.ds(0, 192)

    def stage_one(p, step):
        label = step * 4 if p == 0 else step
        return remote(wg.at[0, p, mine], wg.at[label, p, mine], w1_s.at[p, step], w1_r.at[p, step], peer(label))

    def stage_two(p, source, move):
        to = source + move
        return remote(wg.at[source, p, mine], wg.at[to, p, mine], wq_s.at[p, to], wq_r.at[p, to], peer(move))

    def second_stage(held):
        for step in (1, 3, 2):
            stage_two(0, held * 4, step).start()
            stage_two(1, held, step * 4).start()

    def along_x(label, p, step):
        return remote(
            wg.at[label, p, pl.ds(0, 128)],
            wg.at[label, p, pl.ds(WROW[4 - step] * 128, 128)],
            wx_s.at[label, p, step],
            wx_r.at[label, p, 4 - step],
            xpeer(step),
        )

    def both_ways(label, p):
        for step in (1, 3):
            along_x(label, p, step).start()

    def relay(label):
        up = label % 2
        held = WROW[1] + (WROW[3] - WROW[1]) * up
        return remote(
            wg.at[label, :, pl.ds(pl.multiple_of(held * 128 + 64, 64), 64)],
            wg.at[label, :, pl.ds(WROW[2] * 128 + 64, 64)],
            wx_s.at[label, 0, 2],
            wx_r.at[label, 0, 2],
            xpeer(3 - 2 * up),
        )

    for step in (1, 3, 2):
        for p in range(2):
            stage_one(p, step).start()
    grad_copy = remote(grad_hbm, gbuf.at[1], core_s.at[1], core_r.at[1], partner)
    grad_copy.start()

    reqs[...] = jnp.zeros_like(reqs)
    for k in range(2):
        if k == 1:
            meta_copy.wait_recv()
        flat = metar[k]
        metas[k] = jnp.transpose(jnp.concatenate([flat] * 16, axis=0))
        row = jnp.concatenate([flat[0:1, :], flat[1:2, :]], axis=1).astype(I32)
        owner = row >> 10
        label = ((((owner >> 2) - z) & 3) << 2) | (((owner & 3) - y) & 3)
        hit = label == lax.broadcasted_iota(I32, (16, 1024), 0)
        hits = hot(hit)
        before = []
        for part in range(4):
            upper = lax.broadcasted_iota(I32, (1024, 256), 0) < lax.broadcasted_iota(I32, (1024, 256), 1) + part * 256
            before.append(nn(hits, hot(upper)))
        before = jnp.concatenate(before, axis=1)
        rank = jnp.sum(jnp.where(hit, before, F32(0)), axis=0, keepdims=True)
        slot = label.astype(F32) * 128 + rank
        slotr[k] = jnp.broadcast_to(slot, (8, 1024)).astype(I32)
        slotc[k] = jnp.transpose(jnp.broadcast_to(slot, (128, 1024)))
        rank_column = jnp.transpose(jnp.broadcast_to(rank, (128, 1024)))
        places = hot(rank_column == lax.broadcasted_iota(I32, (1024, 128), 1).astype(F32))
        number = (row & 1023) + 1
        upper_digit = jnp.where(hit, (number >> 5).astype(F32), F32(0)).astype(BF16)
        lower_digit = jnp.where(hit, (number & 31).astype(F32), F32(0)).astype(BF16)
        asked = nn(upper_digit, places) * 32 + nn(lower_digit, places) - 1
        for label_at in range(16):
            reqs[label_at, k : k + 1, :] = asked[label_at : label_at + 1, :]

    def request(label):
        return remote(reqs.at[label], reqr.at[label], req_s.at[label], req_r.at[label], peer(label))

    in_order(lambda label: request(label).start())
    second_stage(0)
    for held in (1, 3, 2):
        for p in range(2):
            stage_one(p, held).wait_recv()
            both_ways(held * 4 if p == 0 else held, p)
        second_stage(held)
    reqr[0] = reqs[0]
    for copy in local_copies:
        copy.wait()

    def value_copy(label, h):
        back = ((z + 4 - label // 4) % 4) * 4 + (y + 4 - label % 4) % 4
        return remote(
            outbox.at[h, :, label], chosen_in.at[h, :, label], val_s.at[h, label], val_r.at[h, label], (back, d)
        )

    def look_up(label, target):
        parts = []
        for k in range(2):
            column = jnp.transpose(jnp.broadcast_to(reqr[label, k : k + 1, :], (128, 128)))
            base = lax.broadcasted_iota(I32, (128, 128), 1).astype(F32)
            parts.append(jnp.concatenate([hot(column == base + 128 * part) for part in range(8)], axis=1))
        found = nn(jnp.concatenate(parts, axis=0), vh[...]).astype(BF16)
        for k in range(2):
            for h in range(2):
                target[h, k, label] = found[k * 128 : (k + 1) * 128, h * 256 : (h + 1) * 256]

    def serve(label):
        request(label).wait_recv()
        look_up(label, outbox)
        value_copy(label, 0).start()

    in_order(serve)
    look_up(0, chosen_in)

    def choose(at, h):
        k, tile = at // 2, at % 2
        column = slotc[k, pl.ds(pl.multiple_of(tile * 512, 512), 512), :]
        base = lax.broadcasted_iota(I32, (512, 128), 1).astype(F32)
        table = jnp.concatenate([hot(column == base + 128 * part) for part in range(16)], axis=1)
        rows = nn(table, chosen_in[h, k].reshape(2048, 256))
        chosen[k, pl.ds(pl.multiple_of(tile * 512, 512), 512), pl.ds(h * 256, 256)] = rows.astype(BF16)

    def mix_half(mt, h):
        half = pl.ds(h * 256, 256)
        for k in range(2):

            def mix(tile):
                here = pl.ds(pl.multiple_of(tile * 128, 128), 128)
                first = chosen[k, here, half].astype(F32)
                second = chosen[k, pl.ds(pl.multiple_of(512 + tile * 128, 128), 128), half].astype(F32)
                for p in range(2):
                    w0 = jnp.where(metas[k, here, 2:3] == p, metas[k, here, 4:5], F32(0))
                    w1 = jnp.where(metas[k, here, 3:4] == p, metas[k, here, 5:6], F32(0))
                    turned = jnp.transpose(w0 * first + w1 * second).astype(BF16)
                    for q in range(2):
                        mt[
                            pl.ds(q * 256 + p * 128, 128),
                            pl.ds(pl.multiple_of(k * 512 + tile * 128, 128), 128),
                        ] = turned[q * 128 : (q + 1) * 128]

            loop(4, mix)

        for a in (0, 2, 1, 3):

            def partial(b):
                columns = pl.ds(pl.multiple_of((((z + a) % 4) * 4 + (y + b) % 4) * 256, 256), 256)
                term = nn(mt[:, :512], gbuf[0, :, columns]) + nn(mt[:, 512:], gbuf[1, :, columns])
                term = term.astype(BF16)
                for q in range(2):
                    pb[JORDER[h * 2 + q], a * 4 + b] = term[q * 256 : (q + 1) * 256]

            loop(4, partial)
            if h == 0:
                two_away(a).start()
            elif a >= 2:
                to_right(a).start()
        if h == 0:
            to_left(0).start()
            to_left(1).start()

    def span(a):
        return pl.ds(a * 4, 4)

    def two_away(a):
        if a < 2:
            return remote(pb.at[2, span(a)], ra.at[span(a)], p2_s.at[a], p2_r.at[a], xpeer(1))
        return remote(pb.at[2, span(a)], rb.at[span(a - 2)], p2_s.at[a], p2_r.at[a], xpeer(3))

    def to_right(a):
        return remote(pb.at[1, span(a)], rl.at[span(a)], p1_s.at[a], p1_r.at[a], xpeer(1))

    def to_left(a):
        return remote(pb.at[3, span(a)], rr.at[span(a)], p3_s.at[a], p3_r.at[a], xpeer(3))

    def values_half(h):
        in_order(lambda label: value_copy(label, h).wait_recv())
        loop(4, lambda at: choose(at, h))
        pl.run_scoped(lambda mt: mix_half(mt, h), pltpu.VMEM((512, 1024), BF16))

    def merge(a):
        two_away(a).wait_recv()
        block, arrived, shift = (1, ra, 0) if a < 2 else (3, rb, 8)

        def add(b):
            at = a * 4 + b
            pb[block, at] = (pb[block, at].astype(F32) + arrived[at - shift].astype(F32)).astype(BF16)

        loop(4, add)
        (to_right(a) if a < 2 else to_left(a)).start()

    def contrib_copy(label, h):
        return remote(
            outbox.at[h, :, label], contrib_in.at[h, :, label], con_s.at[h, label], con_r.at[h, label], peer(label)
        )

    def score_copy():
        return remote(sgs.at[1], sgr, core_s.at[2], core_r.at[2], partner)

    def scope_pick(pr, contrib):
        def columns_of(label):
            return pl.ds(pl.multiple_of(peer_from(label) * 256, 256), 256)

        def peer_from(label):
            return ((z + 4 - label // 4) % 4) * 4 + (y + 4 - label % 4) % 4

        def project(label, j, first=False):
            place = PLACE[j] * 128
            rows = pl.ds(WROW[j] * 128, 128)
            weights = jnp.concatenate([wg[label, 0, rows], wg[label, 1, rows]], axis=0)
            for k in range(2):
                term = nt(gbuf[k, :, columns_of(label)], weights)
                for p in range(2):
                    here = (pl.ds(k * 512, 512), pl.ds(p * 512 + place, 128))
                    part = term[:, p * 128 : (p + 1) * 128]
                    pr[here] = part if first else pr[here] + part

        def picked(k, q, tile):
            here = pl.ds(pl.multiple_of(tile * 128, 128), 128)
            wide = pr[pl.ds(pl.multiple_of(k * 512 + tile * 128, 128), 128), :]
            return jnp.where(metas[k, here, 2 + q : 3 + q] == 0, wide[:, :512], wide[:, 512:])

        def forward(label):
            @pl.when(label % 4 != 0)
            def _():
                stage_two(0, label, 0).wait_recv()
                both_ways(label, 0)

            @pl.when(label // 4 != 0)
            def _():
                stage_two(1, label, 0).wait_recv()
                both_ways(label, 1)

            project(label, 0)

        def pass_on(label):
            for p in range(2):
                for step in (1, 3):
                    along_x(label, p, step).wait_recv()
            relay(label).start()
            for j in (1, 3):
                project(label, j)

        def last(label):
            relay(label).wait_recv()
            project(label, 2)

        grad_copy.wait_recv()
        for j in range(4):
            project(0, j, True)
        in_order(forward)
        in_order(lambda label: value_copy(label, 1).start())
        in_order(pass_on)
        values_half(0)
        in_order(last)

        for k in range(2):

            def pick(tile):
                here = pl.ds(pl.multiple_of(tile * 128, 128), 128)
                for q in range(2):
                    rows = pl.ds(pl.multiple_of(q * 512 + tile * 128, 128), 128)
                    contrib[k, rows, :] = (metas[k, here, 4 + q : 5 + q] * picked(k, q, tile)).astype(BF16)

            loop(4, pick)

        def pack(label, h, target):
            for k in range(2):
                places = lax.broadcasted_iota(I32, (128, 1024), 0) + label * 128
                half = contrib[k, :, pl.ds(h * 256, 256)]
                target[h, k, label] = nn(hot(slotr[k, 0:1, :] == places), half).astype(BF16)

        def send(label, h):
            pack(label, h, outbox)
            contrib_copy(label, h).start()

        in_order(lambda label: value_copy(label, 0).wait_send())
        in_order(lambda label: send(label, 0))
        values_half(1)
        in_order(lambda label: value_copy(label, 1).wait_send())
        in_order(lambda label: send(label, 1))
        for h in range(2):
            pack(0, h, contrib_in)
        for a in (1, 2, 0, 3):
            merge(a)

        for k in range(2):

            def score(tile):
                lanes = lax.broadcasted_iota(I32, (128, 128), 1)
                kept = jnp.zeros((128, 128), F32)
                for q in range(2):
                    rows = pl.ds(pl.multiple_of(q * 512 + tile * 128, 128), 128)
                    total = jnp.sum(picked(k, q, tile) * chosen[k, rows, :].astype(F32), axis=1, keepdims=True)
                    kept = jnp.where(lanes == q, total, kept)
                sgs[k, pl.ds(pl.multiple_of(tile * 128, 128), 128), :] = kept

            loop(4, score)
        score_copy().start()

    pl.run_scoped(scope_pick, pltpu.VMEM((1024, 1024), F32), pltpu.VMEM((2, 1024, 512), BF16))

    def half_rows(p):
        return pl.ds(p * 128, 128)

    def first_z(a):
        return remote(pb.at[0, span(a), half_rows(0)], f1.at[0, a], f1_s.at[0, a, 0], f1_r.at[0, a, 0], peer(a * 4))

    def first_y(a, b):
        return remote(pb.at[0, a * 4 + b, half_rows(1)], f1.at[1, b, a], f1_s.at[1, b, a], f1_r.at[1, b, a], peer(b))

    def then_y(b):
        return remote(pb.at[0, b, half_rows(0)], f2.at[0, b], f2_s.at[0, b], f2_r.at[0, b], peer(b))

    def then_z(a):
        return remote(pb.at[0, a * 4, half_rows(1)], f2.at[1, a], f2_s.at[1, a], f2_r.at[1, a], peer(a * 4))

    def finish_x(order):
        for a in order:
            to_right(a).wait_recv()
            to_left(a).wait_recv()

            def finish(b):
                at = a * 4 + b
                total = pb[0, at].astype(F32) + rl[at].astype(F32) + rr[at].astype(F32)
                pb[0, at] = total.astype(BF16)

            loop(4, finish)
            if a:
                first_z(a).start()
            for b in (1, 3, 2):
                first_y(a, b).start()

    def finish_stage():
        for step in (1, 3, 2):
            first_z(step).wait_recv()
            for a in range(4):
                first_y(a, step).wait_recv()
        for place in (1, 3, 2, 0):
            for p in range(2):
                at = place if p == 0 else place * 4
                total = pb[0, at, half_rows(p), :].astype(F32)
                for step in range(1, 4):
                    total = total + f1[p, step, place].astype(F32)
                pb[0, at, half_rows(p), :] = total.astype(BF16)
            if place:
                then_y(place).start()
                then_z(place).start()

    def vg_copy(step, h):
        return remote(vgs.at[h, step], vgr.at[h, step], vx_s.at[h, step], vx_r.at[h, step], xpeer(step))

    def vg_partner():
        return remote(vgp_s, vgp_r, core_s.at[3], core_r.at[3], partner)

    def scope_values(vg):
        def gather(label, h, first=False):
            half = pl.ds(h * 256, 256)
            parts = []
            for k in range(2):
                places = lax.broadcasted_iota(I32, (1024, 128), 0).astype(F32)
                parts.append(hot(places == reqr[label, k : k + 1, :]))
            rows = jnp.concatenate([contrib_in[h, 0, label], contrib_in[h, 1, label]], axis=0)
            term = nn(jnp.concatenate(parts, axis=1), rows)
            vg[:, half] = term if first else vg[:, half] + term

        for h in range(2):
            gather(0, h, True)

            def arrive(label):
                contrib_copy(label, h).wait_recv()
                gather(label, h)

            in_order(arrive)
            for step in (2, 1, 3):
                rows = pl.ds(pl.multiple_of(((x + step) % 4) * 256, 256), 256)
                vgs[h, step] = vg[rows, pl.ds(h * 256, 256)].astype(BF16)
                vg_copy(step, h).start()
        finish_x((2, 1, 3, 0))
        finish_stage()
        vg[:256, :] = vg[pl.ds(pl.multiple_of(x * 256, 256), 256), :]
        for h in range(2):
            for step in (1, 3, 2):
                vg_copy(step, h).wait_recv()
                for q in range(2):
                    to = pl.ds(PLACE[(JORDER[h * 2 + q] - step) % 4] * 128, 128)
                    vg[:256, to] = vg[:256, to] + vgr[h, step, :, pl.ds(q * 128, 128)].astype(F32)
        vgp_s[...] = vg[pl.ds(pl.multiple_of((1 - c) * 128, 128), 128), :].astype(BF16)
        vg_partner().start()
        mine = vg[pl.ds(pl.multiple_of(c * 128, 128), 128), :].astype(BF16)
        for q in range(4):
            at = pl.multiple_of(((x + JORDER[q]) % 4) * 256 + c * 128, 128)
            vg_out[:, pl.ds(at, 128)] = mine[:, q * 128 : (q + 1) * 128]

    pl.run_scoped(scope_values, pltpu.VMEM((1024, 512), F32))

    for step in (1, 3, 2):
        then_y(step).wait_recv()
        then_z(step).wait_recv()
    for p in range(2):
        total = pb[0, 0, half_rows(p), :].astype(F32)
        for step in range(1, 4):
            total = total + f2[p, step].astype(F32)
        pg_out[p] = total

    score_copy().wait_recv()
    sg_out[...] = jnp.transpose(sgs[0] + sgr[...])[0:2, :]

    vg_partner().wait_recv()
    other = vgp_r[...]
    for q in range(4):
        at = pl.multiple_of(((x + JORDER[q]) % 4) * 256 + (1 - c) * 128, 128)
        vg_out[:, pl.ds(at, 128)] = other[:, q * 128 : (q + 1) * 128]

    meta_copy.wait_send()
    grad_copy.wait_send()
    score_copy().wait_send()
    vg_partner().wait_send()

    def sent(label):
        @pl.when(label % 4 != 0)
        def _():
            stage_two(0, label, 0).wait_send()

        @pl.when(label // 4 != 0)
        def _():
            stage_two(1, label, 0).wait_send()

        request(label).wait_send()
        for h in range(2):
            contrib_copy(label, h).wait_send()
        for p in range(2):
            for step in (1, 3):
                along_x(label, p, step).wait_send()
        relay(label).wait_send()

    loop(16, sent, 1)
    for step in range(1, 4):
        for h in range(2):
            vg_copy(step, h).wait_send()
        first_z(step).wait_send()
        for p in range(2):
            stage_one(p, step).wait_send()
        then_y(step).wait_send()
        then_z(step).wait_send()
        for a in range(4):
            first_y(a, step).wait_send()
    for a in range(4):
        two_away(a).wait_send()
        to_right(a).wait_send()
        to_left(a).wait_send()


def local(grad_out, scores, row_ids, proj_ids, values, proj_w):
    vmem = pl.BlockSpec(memory_space=pltpu.VMEM)
    anywhere = pl.BlockSpec(memory_space=pl.ANY)
    dma = pltpu.SemaphoreType.DMA
    score_grads, value_grads, proj_grads = pl.pallas_call(
        kernel,
        out_shape=(
            jax.ShapeDtypeStruct((2, 512), F32),
            jax.ShapeDtypeStruct((128, 1024), BF16),
            jax.ShapeDtypeStruct((2, 128, 256), F32),
        ),
        in_specs=[anywhere, vmem, vmem, vmem, anywhere, anywhere],
        out_specs=(vmem, vmem, vmem),
        scratch_shapes=[
            pltpu.VMEM((2, 512, 4096), BF16),
            pltpu.VMEM((16, 2, 512, 256), BF16),
            pltpu.VMEM((1024, 512), BF16),
            pltpu.VMEM((2, 2, 16, 128, 256), BF16),
            pltpu.VMEM((2, 2, 16, 128, 256), BF16),
            pltpu.VMEM((2, 2, 16, 128, 256), BF16),
            pltpu.VMEM((2, 1024, 512), BF16),
            pltpu.VMEM((4, 16, 256, 256), BF16),
            pltpu.VMEM((8, 256, 256), BF16),
            pltpu.VMEM((8, 256, 256), BF16),
            pltpu.VMEM((16, 256, 256), BF16),
            pltpu.VMEM((16, 256, 256), BF16),
            pltpu.VMEM((2, 4, 4, 128, 256), BF16),
            pltpu.VMEM((2, 4, 128, 256), BF16),
            pltpu.VMEM((2, 4, 256, 256), BF16),
            pltpu.VMEM((2, 4, 256, 256), BF16),
            pltpu.VMEM((128, 512), BF16),
            pltpu.VMEM((128, 512), BF16),
            pltpu.VMEM((2, 8, 512), F32),
            pltpu.VMEM((2, 512, 128), F32),
            pltpu.VMEM((2, 8, 1024), I32),
            pltpu.VMEM((2, 1024, 128), F32),
            pltpu.VMEM((16, 8, 128), F32),
            pltpu.VMEM((16, 8, 128), F32),
            pltpu.VMEM((2, 512, 128), F32),
            pltpu.VMEM((512, 128), F32),
            dma((13,)),
            dma((4,)),
            dma((4,)),
            dma((16,)),
            dma((16,)),
            dma((2, 16)),
            dma((2, 16)),
            dma((2, 4)),
            dma((2, 4)),
            dma((2, 16)),
            dma((2, 16)),
            dma((16, 2, 4)),
            dma((16, 2, 4)),
            dma((4,)),
            dma((4,)),
            dma((4,)),
            dma((4,)),
            dma((4,)),
            dma((4,)),
            dma((2, 16)),
            dma((2, 16)),
            dma((2, 4, 4)),
            dma((2, 4, 4)),
            dma((2, 4)),
            dma((2, 4)),
            dma((2, 4)),
            dma((2, 4)),
        ],
        compiler_params=pltpu.CompilerParams(
            collective_id=0, has_side_effects=True, vmem_limit_bytes=67043328
        ),
        name="step",
    )(grad_out, scores.T, row_ids.T, proj_ids.T, values, proj_w.reshape(2, 4, 2, 128, 256))
    return score_grads.T, value_grads, proj_grads


def solution(mesh):
    return jax.shard_map(
        local,
        mesh=mesh,
        in_specs=(
            P(("mem", "dp"), None),
            P(("mem", "dp"), None),
            P(("mem", "dp"), None),
            P(("mem", "dp"), None),
            P("mem", None),
            P(None, None, "mem"),
        ),
        out_specs=(P(("mem", "dp"), None), P(("mem", "dp"), None), P(None, "dp", "mem")),
        check_vma=False,
    )
```

time: 240 us -> 167 us (0.70); the launches traced: 237 us -> 167 us
  Pallas kernels: 226 us -> 161 us
  local copies, waits for them, and re-layouts: 9.6 us -> 4.6 us
    pallas_call x1, Pallas kernels: 226 us -> 161 us  [local(): pl.pallas_call(kernel, out_shape=(jax.ShapeDtypeStruct((2, 512), F32), ja...]
    unnamed x5 -> x3, local copies, waits for them, and re-layouts: 7.95 us -> 4.6 us
where the time goes in v2:
time: 167 us
  Pallas kernels  161 us (96%)
  local copies, waits for them, and re-layouts  4.6 us (3%)
    pallas_call x1, Pallas kernels, local(): pl.pallas_call(kernel, out_shape=(jax.ShapeDtypeStruct((2, 512), F32), ja...  161 us
    unnamed x3, local copies, waits for them, and re-layouts  4.6 us

profile of v2, /device:TPU:0, one launch (start us, length us, event | category | flops | bytes accessed | tf_op | source)
XLA Modules:
  0.0 166.6 jit_solution(5547334629631066816)
XLA Ops:
  0.6 161.3 %step.1 = (f32[2,512]{1,0:T(2,128)}, bf16[128,1024]{1,0:T(8,128)(2,1)}, f32[2,128,256]{2,1,0:T(8,128)}) custom-call(bf16[512,4096]{1,0:T(8,128)(2,1)} %grad_hbm.1, f32[2,512]{1,0:T(2,128)} %bitcast.6, s32[2,512]{1,0:T(2,128)} %bitcast.7, s32[2,512]{1,0:T(2,128)} %bitcast.8, bf16[1024,1024]{1,0:T(8,128)(2,1)} %values_hbm.1, bf16[2,4,2,128,256]{4,3,2,1,0:T(8,128)(2,1)} %bitcast.5), custom_call_target="tpu_custom_call" | custom-call | tf_op jit(solution)/shard_map/step/pallas_call | solution.py:570
  162.0 1.3 copy.12
  163.2 1.7 %copy.13 = bf16[128,1024]{1,0:T(8,128)(2,1)} copy(bf16[128,1024]{1,0:T(8,128)(2,1)} %get-tuple-element.13) | data formatting | bytes 524288
  164.9 1.7 %copy.14 = f32[2,128,256]{2,1,0:T(8,128)} copy(f32[2,128,256]{2,1,0:T(8,128)} %get-tuple-element.14) | data formatting | bytes 524288

commit v3 on v2

--- a/solution.py
+++ b/solution.py
@@ -51,8 +51,8 @@
     sg_out, vg_out, pg_out,
     gbuf, wg, vh, outbox, chosen_in, contrib_in, chosen, pb, ra, rb, rl, rr, f1, f2,
     vgs, vgr, vgp_s, vgp_r, metar, metas, slotr, slotc, reqs, reqr, sgs, sgr,
-    lsem, core_s, core_r, req_s, req_r, val_s, val_r, w1_s, w1_r, wq_s, wq_r, wx_s, wx_r,
-    p2_s, p2_r, p1_s, p1_r, p3_s, p3_r, con_s, con_r, f1_s, f1_r, f2_s, f2_r, vx_s, vx_r,
+    lsem, core_s, core_r, out_s, req_r, val_s, val_r, w1_r, wq_r, wx_r, rel_r,
+    p2_r, p1_r, p3_r, con_s, con_r, f1_r, f2_r, vx_s, vx_r,
 ):
     m = lax.axis_index("mem")
     d = lax.axis_index("dp")
@@ -81,7 +81,7 @@
             pltpu.make_async_copy(
                 values_hbm.at[:, pl.ds(pl.multiple_of(block * 256 + c * 128, 128), 128)],
                 vh.at[:, pl.ds(q * 128, 128)],
-                lsem.at[1 + q],
+                lsem.at[2],
             )
         )
     w_copies = []
@@ -89,7 +89,7 @@
         for q in range(4):
             w_copies.append(
                 pltpu.make_async_copy(
-                    w_hbm.at[p, (x + JORDER[q]) % 4, c], wg.at[0, p, pl.ds(WROW[JORDER[q]] * 128, 128)], lsem.at[5 + p * 4 + q]
+                    w_hbm.at[p, (x + JORDER[q]) % 4, c], wg.at[0, p, pl.ds(WROW[JORDER[q]] * 128, 128)], lsem.at[1]
                 )
             )
     for copy in w_copies + local_copies:
@@ -109,18 +109,17 @@
 
     meta_copy = remote(metar.at[0], metar.at[1], core_s.at[0], core_r.at[0], partner)
     meta_copy.start()
-    for copy in w_copies:
-        copy.wait()
+    pltpu.make_async_copy(wg.at[0], wg.at[0], lsem.at[1]).wait()
 
     mine = pl.ds(0, 192)
 
     def stage_one(p, step):
         label = step * 4 if p == 0 else step
-        return remote(wg.at[0, p, mine], wg.at[label, p, mine], w1_s.at[p, step], w1_r.at[p, step], peer(label))
+        return remote(wg.at[0, p, mine], wg.at[label, p, mine], out_s.at[0], w1_r.at[p, step], peer(label))
 
     def stage_two(p, source, move):
         to = source + move
-        return remote(wg.at[source, p, mine], wg.at[to, p, mine], wq_s.at[p, to], wq_r.at[p, to], peer(move))
+        return remote(wg.at[source, p, mine], wg.at[to, p, mine], out_s.at[0], wq_r.at[p, to], peer(move))
 
     def second_stage(held):
         for step in (1, 3, 2):
@@ -131,10 +130,14 @@
         return remote(
             wg.at[label, p, pl.ds(0, 128)],
             wg.at[label, p, pl.ds(WROW[4 - step] * 128, 128)],
-            wx_s.at[label, p, step],
-            wx_r.at[label, p, 4 - step],
+            out_s.at[1],
+            wx_r.at[label],
             xpeer(step),
         )
+
+    def from_both(label):
+        block = wg.at[label, :, pl.ds(256, 256)]
+        return remote(block, block, out_s.at[1], wx_r.at[label], xpeer(1))
 
     def both_ways(label, p):
         for step in (1, 3):
@@ -146,8 +149,8 @@
         return remote(
             wg.at[label, :, pl.ds(pl.multiple_of(held * 128 + 64, 64), 64)],
             wg.at[label, :, pl.ds(WROW[2] * 128 + 64, 64)],
-            wx_s.at[label, 0, 2],
-            wx_r.at[label, 0, 2],
+            out_s.at[2],
+            rel_r.at[label],
             xpeer(3 - 2 * up),
         )
 
@@ -187,7 +190,7 @@
             reqs[label_at, k : k + 1, :] = asked[label_at : label_at + 1, :]
 
     def request(label):
-        return remote(reqs.at[label], reqr.at[label], req_s.at[label], req_r.at[label], peer(label))
+        return remote(reqs.at[label], reqr.at[label], out_s.at[3], req_r.at[label], peer(label))
 
     in_order(lambda label: request(label).start())
     second_stage(0)
@@ -197,14 +200,18 @@
             both_ways(held * 4 if p == 0 else held, p)
         second_stage(held)
     reqr[0] = reqs[0]
-    for copy in local_copies:
-        copy.wait()
+    local_copies[0].wait()
+    pltpu.make_async_copy(vh, vh, lsem.at[2]).wait()
 
     def value_copy(label, h):
         back = ((z + 4 - label // 4) % 4) * 4 + (y + 4 - label % 4) % 4
         return remote(
-            outbox.at[h, :, label], chosen_in.at[h, :, label], val_s.at[h, label], val_r.at[h, label], (back, d)
+            outbox.at[h, :, label], chosen_in.at[h, :, label], val_s.at[h], val_r.at[h], (back, d)
         )
+
+    def all_values(h):
+        every = pl.ds(1, 15)
+        return remote(outbox.at[h, :, every], chosen_in.at[h, :, every], val_s.at[h], val_r.at[h], partner)
 
     def look_up(label, target):
         parts = []
@@ -276,17 +283,17 @@
 
     def two_away(a):
         if a < 2:
-            return remote(pb.at[2, span(a)], ra.at[span(a)], p2_s.at[a], p2_r.at[a], xpeer(1))
-        return remote(pb.at[2, span(a)], rb.at[span(a - 2)], p2_s.at[a], p2_r.at[a], xpeer(3))
+            return remote(pb.at[2, span(a)], ra.at[span(a)], out_s.at[4], p2_r.at[a], xpeer(1))
+        return remote(pb.at[2, span(a)], rb.at[span(a - 2)], out_s.at[4], p2_r.at[a], xpeer(3))
 
     def to_right(a):
-        return remote(pb.at[1, span(a)], rl.at[span(a)], p1_s.at[a], p1_r.at[a], xpeer(1))
+        return remote(pb.at[1, span(a)], rl.at[span(a)], out_s.at[5], p1_r.at[a], xpeer(1))
 
     def to_left(a):
-        return remote(pb.at[3, span(a)], rr.at[span(a)], p3_s.at[a], p3_r.at[a], xpeer(3))
+        return remote(pb.at[3, span(a)], rr.at[span(a)], out_s.at[6], p3_r.at[a], xpeer(3))
 
     def values_half(h):
-        in_order(lambda label: value_copy(label, h).wait_recv())
+        all_values(h).wait_recv()
         loop(4, lambda at: choose(at, h))
         pl.run_scoped(lambda mt: mix_half(mt, h), pltpu.VMEM((512, 1024), BF16))
 
@@ -303,7 +310,7 @@
 
     def contrib_copy(label, h):
         return remote(
-            outbox.at[h, :, label], contrib_in.at[h, :, label], con_s.at[h, label], con_r.at[h, label], peer(label)
+            outbox.at[h, :, label], contrib_in.at[h, :, label], con_s.at[h], con_r.at[h, label], peer(label)
         )
 
     def score_copy():
@@ -346,9 +353,7 @@
             project(label, 0)
 
         def pass_on(label):
-            for p in range(2):
-                for step in (1, 3):
-                    along_x(label, p, step).wait_recv()
+            from_both(label).wait_recv()
             relay(label).start()
             for j in (1, 3):
                 project(label, j)
@@ -386,10 +391,10 @@
             pack(label, h, outbox)
             contrib_copy(label, h).start()
 
-        in_order(lambda label: value_copy(label, 0).wait_send())
+        all_values(0).wait_send()
         in_order(lambda label: send(label, 0))
         values_half(1)
-        in_order(lambda label: value_copy(label, 1).wait_send())
+        all_values(1).wait_send()
         in_order(lambda label: send(label, 1))
         for h in range(2):
             pack(0, h, contrib_in)
@@ -416,51 +421,71 @@
         return pl.ds(p * 128, 128)
 
     def first_z(a):
-        return remote(pb.at[0, span(a), half_rows(0)], f1.at[0, a], f1_s.at[0, a, 0], f1_r.at[0, a, 0], peer(a * 4))
+        return remote(pb.at[0, span(a), half_rows(0)], f1.at[0, a], out_s.at[7], f1_r.at[4], peer(a * 4))
 
     def first_y(a, b):
-        return remote(pb.at[0, a * 4 + b, half_rows(1)], f1.at[1, b, a], f1_s.at[1, b, a], f1_r.at[1, b, a], peer(b))
+        return remote(pb.at[0, a * 4 + b, half_rows(1)], f1.at[1, b, a], out_s.at[8], f1_r.at[a], peer(b))
 
     def then_y(b):
-        return remote(pb.at[0, b, half_rows(0)], f2.at[0, b], f2_s.at[0, b], f2_r.at[0, b], peer(b))
+        return remote(pb.at[0, b, half_rows(0)], f2.at[0, b], out_s.at[9], f2_r.at[0], peer(b))
 
     def then_z(a):
-        return remote(pb.at[0, a * 4, half_rows(1)], f2.at[1, a], f2_s.at[1, a], f2_r.at[1, a], peer(a * 4))
-
-    def finish_x(order):
-        for a in order:
-            to_right(a).wait_recv()
-            to_left(a).wait_recv()
-
-            def finish(b):
-                at = a * 4 + b
-                total = pb[0, at].astype(F32) + rl[at].astype(F32) + rr[at].astype(F32)
-                pb[0, at] = total.astype(BF16)
-
-            loop(4, finish)
-            if a:
-                first_z(a).start()
-            for b in (1, 3, 2):
-                first_y(a, b).start()
-
-    def finish_stage():
-        for step in (1, 3, 2):
-            first_z(step).wait_recv()
-            for a in range(4):
-                first_y(a, step).wait_recv()
-        for place in (1, 3, 2, 0):
-            for p in range(2):
-                at = place if p == 0 else place * 4
-                total = pb[0, at, half_rows(p), :].astype(F32)
-                for step in range(1, 4):
-                    total = total + f1[p, step, place].astype(F32)
-                pb[0, at, half_rows(p), :] = total.astype(BF16)
-            if place:
-                then_y(place).start()
-                then_z(place).start()
+        return remote(pb.at[0, a * 4, half_rows(1)], f2.at[1, a], out_s.at[10], f2_r.at[1], peer(a * 4))
+
+    others = pl.ds(1, 3)
+
+    def all_first_z():
+        block = f1.at[0, others]
+        return remote(block, block, out_s.at[7], f1_r.at[4], partner)
+
+    def all_first_y(a):
+        block = f1.at[1, others, a]
+        return remote(block, block, out_s.at[8], f1_r.at[a], partner)
+
+    def all_then(p):
+        block = f2.at[p, others]
+        return remote(block, block, out_s.at[9 + p], f2_r.at[p], partner)
+
+    def finish_x(a):
+        to_right(a).wait_recv()
+        to_left(a).wait_recv()
+
+        def finish(b):
+            at = a * 4 + b
+            total = pb[0, at].astype(F32) + rl[at].astype(F32) + rr[at].astype(F32)
+            pb[0, at] = total.astype(BF16)
+
+        loop(4, finish)
+        if a:
+            first_z(a).start()
+        for b in (1, 3, 2):
+            first_y(a, b).start()
+
+    def gathered(p, place):
+        total = pb[0, place if p == 0 else place * 4, half_rows(p), :].astype(F32)
+        for step in range(1, 4):
+            total = total + f1[p, step, place].astype(F32)
+        return total
+
+    def finish_all():
+        for a in (2, 1, 3):
+            finish_x(a)
+        for a in (2, 1, 3):
+            all_first_y(a).wait_recv()
+            pb[0, a * 4, half_rows(1), :] = gathered(1, a).astype(BF16)
+            then_z(a).start()
+        all_first_z().wait_recv()
+        finish_x(0)
+        for b in (1, 3, 2):
+            pb[0, b, half_rows(0), :] = gathered(0, b).astype(BF16)
+            then_y(b).start()
 
     def vg_copy(step, h):
-        return remote(vgs.at[h, step], vgr.at[h, step], vx_s.at[h, step], vx_r.at[h, step], xpeer(step))
+        return remote(vgs.at[h, step], vgr.at[h, step], vx_s.at[h], vx_r.at[h], xpeer(step))
+
+    def all_vg(h):
+        block = vgr.at[h, others]
+        return remote(block, block, vx_s.at[h], vx_r.at[h], partner)
 
     def vg_partner():
         return remote(vgp_s, vgp_r, core_s.at[3], core_r.at[3], partner)
@@ -488,12 +513,11 @@
                 rows = pl.ds(pl.multiple_of(((x + step) % 4) * 256, 256), 256)
                 vgs[h, step] = vg[rows, pl.ds(h * 256, 256)].astype(BF16)
                 vg_copy(step, h).start()
-        finish_x((2, 1, 3, 0))
-        finish_stage()
+        finish_all()
         vg[:256, :] = vg[pl.ds(pl.multiple_of(x * 256, 256), 256), :]
         for h in range(2):
+            all_vg(h).wait_recv()
             for step in (1, 3, 2):
-                vg_copy(step, h).wait_recv()
                 for q in range(2):
                     to = pl.ds(PLACE[(JORDER[h * 2 + q] - step) % 4] * 128, 128)
                     vg[:256, to] = vg[:256, to] + vgr[h, step, :, pl.ds(q * 128, 128)].astype(F32)
@@ -506,11 +530,11 @@
 
     pl.run_scoped(scope_values, pltpu.VMEM((1024, 512), F32))
 
-    for step in (1, 3, 2):
-        then_y(step).wait_recv()
-        then_z(step).wait_recv()
+    all_first_y(0).wait_recv()
     for p in range(2):
-        total = pb[0, 0, half_rows(p), :].astype(F32)
+        all_then(p).wait_recv()
+    for p in range(2):
+        total = gathered(p, 0)
         for step in range(1, 4):
             total = total + f2[p, step].astype(F32)
         pg_out[p] = total
@@ -529,51 +553,42 @@
     score_copy().wait_send()
     vg_partner().wait_send()
 
-    def sent(label):
-        @pl.when(label % 4 != 0)
-        def _():
-            stage_two(0, label, 0).wait_send()
-
-        @pl.when(label // 4 != 0)
-        def _():
-            stage_two(1, label, 0).wait_send()
-
-        request(label).wait_send()
-        for h in range(2):
-            contrib_copy(label, h).wait_send()
-        for p in range(2):
-            for step in (1, 3):
-                along_x(label, p, step).wait_send()
-        relay(label).wait_send()
-
-    loop(16, sent, 1)
-    for step in range(1, 4):
-        for h in range(2):
-            vg_copy(step, h).wait_send()
-        first_z(step).wait_send()
-        for p in range(2):
-            stage_one(p, step).wait_send()
-        then_y(step).wait_send()
-        then_z(step).wait_send()
-        for a in range(4):
-            first_y(a, step).wait_send()
-    for a in range(4):
-        two_away(a).wait_send()
-        to_right(a).wait_send()
-        to_left(a).wait_send()
+    def drain(block, sem):
+        remote(block, block, sem, w1_r.at[0, 0], partner).wait_send()
+
+    drain(wg.at[pl.ds(1, 15), :, mine], out_s.at[0])
+    drain(wg.at[pl.ds(1, 15), :, pl.ds(256, 256)], out_s.at[1])
+    drain(wg.at[pl.ds(1, 15), :, pl.ds(192, 64)], out_s.at[2])
+    drain(reqs.at[pl.ds(1, 15)], out_s.at[3])
+    for block in (2, 1, 3):
+        drain(pb.at[block], out_s.at[4 + (2, 1, 3).index(block)])
+    drain(f1.at[0, others], out_s.at[7])
+    drain(f1.at[1, :, others], out_s.at[8])
+    for p in range(2):
+        drain(f2.at[p, others], out_s.at[9 + p])
+    for h in range(2):
+        drain(contrib_in.at[h, :, pl.ds(1, 15)], con_s.at[h])
+        drain(vgr.at[h, others], vx_s.at[h])
+
+
+def hand_over(sg_in, vg_in, pg_in, sg_out, vg_out, pg_out):
+    sg_out[...] = sg_in[...]
+    vg_out[...] = vg_in[...]
+    pg_out[...] = pg_in[...]
 
 
 def local(grad_out, scores, row_ids, proj_ids, values, proj_w):
     vmem = pl.BlockSpec(memory_space=pltpu.VMEM)
     anywhere = pl.BlockSpec(memory_space=pl.ANY)
     dma = pltpu.SemaphoreType.DMA
-    score_grads, value_grads, proj_grads = pl.pallas_call(
+    shapes = (
+        jax.ShapeDtypeStruct((2, 512), F32),
+        jax.ShapeDtypeStruct((128, 1024), BF16),
+        jax.ShapeDtypeStruct((2, 128, 256), F32),
+    )
+    results = pl.pallas_call(
         kernel,
-        out_shape=(
-            jax.ShapeDtypeStruct((2, 512), F32),
-            jax.ShapeDtypeStruct((128, 1024), BF16),
-            jax.ShapeDtypeStruct((2, 128, 256), F32),
-        ),
+        out_shape=shapes,
         in_specs=[anywhere, vmem, vmem, vmem, anywhere, anywhere],
         out_specs=(vmem, vmem, vmem),
         scratch_shapes=[
@@ -603,39 +618,35 @@
             pltpu.VMEM((16, 8, 128), F32),
             pltpu.VMEM((2, 512, 128), F32),
             pltpu.VMEM((512, 128), F32),
-            dma((13,)),
+            dma((3,)),
             dma((4,)),
             dma((4,)),
+            dma((11,)),
+            dma((16,)),
+            dma((2,)),
+            dma((2,)),
+            dma((2, 4)),
+            dma((2, 16)),
             dma((16,)),
             dma((16,)),
-            dma((2, 16)),
-            dma((2, 16)),
-            dma((2, 4)),
-            dma((2, 4)),
-            dma((2, 16)),
-            dma((2, 16)),
-            dma((16, 2, 4)),
-            dma((16, 2, 4)),
             dma((4,)),
             dma((4,)),
             dma((4,)),
-            dma((4,)),
-            dma((4,)),
-            dma((4,)),
+            dma((2,)),
             dma((2, 16)),
-            dma((2, 16)),
-            dma((2, 4, 4)),
-            dma((2, 4, 4)),
-            dma((2, 4)),
-            dma((2, 4)),
-            dma((2, 4)),
-            dma((2, 4)),
+            dma((5,)),
+            dma((2,)),
+            dma((2,)),
+            dma((2,)),
         ],
         compiler_params=pltpu.CompilerParams(
             collective_id=0, has_side_effects=True, vmem_limit_bytes=67043328
         ),
         name="step",
     )(grad_out, scores.T, row_ids.T, proj_ids.T, values, proj_w.reshape(2, 4, 2, 128, 256))
+    score_grads, value_grads, proj_grads = pl.pallas_call(
+        hand_over, out_shape=shapes, in_specs=[vmem] * 3, out_specs=(vmem,) * 3, name="hand_over"
+    )(*results)
     return score_grads.T, value_grads, proj_grads
 
 

time: 167 us -> 160 us (0.958)
  local copies, waits for them, and re-layouts: 4.6 us -> 0 us
  Pallas kernels: 161 us -> 157 us
    unnamed x3 -> x0, local copies, waits for them, and re-layouts: 4.6 us -> none
    pallas_call x1 -> x2, Pallas kernels: 161 us -> 157 us  [the longest x1 156 us: local(): pl.pallas_call(kernel, out_shape=shapes, in_specs=[anywhere, vmem, vmem,...]
where the time goes in v3:
time: 160 us; the launch traced here: 158 us
  Pallas kernels  157 us (98%)
    pallas_call x1, Pallas kernels, local(): pl.pallas_call(kernel, out_shape=shapes, in_specs=[anywhere, vmem, vmem,...  156 us

profile of v3, /device:TPU:0, one launch (start us, length us, event | category | flops | bytes accessed | tf_op | source)
XLA Modules:
  0.0 158.1 jit_solution(17277297928741722930)
XLA Ops:
  0.6 155.6 %step.1 = (f32[2,512]{1,0:T(2,128)}, bf16[128,1024]{1,0:T(8,128)(2,1)}, f32[2,128,256]{2,1,0:T(8,128)}) custom-call(bf16[512,4096]{1,0:T(8,128)(2,1)} %grad_hbm.1, f32[2,512]{1,0:T(2,128)} %bitcast.6, s32[2,512]{1,0:T(2,128)} %bitcast.7, s32[2,512]{1,0:T(2,128)} %bitcast.8, bf16[1024,1024]{1,0:T(8,128)(2,1)} %values_hbm.1, bf16[2,4,2,128,256]{4,3,2,1,0:T(8,128)(2,1)} %bitcast.5), custom_call_target="tpu_custom_call" | custom-call | tf_op jit(solution)/shard_map/step/pallas_call | solution.py:589
  156.3 1.8 %hand_over.1 = (f32[2,512]{1,0:T(2,128)}, bf16[128,1024]{1,0:T(8,128)(2,1)}, f32[2,128,256]{2,1,0:T(8,128)}) custom-call(f32[2,512]{1,0:T(2,128)} %get-tuple-element.9.sg_in, bf16[128,1024]{1,0:T(8,128)(2,1)} %get-tuple-element.10.vg_in, f32[2,128,256]{2,1,0:T(8,128)} %get-tuple-element.11.pg_in), custom_call_target="tpu_custom_call" | custom-call | tf_op jit(solution)/shard_map/hand_over/pallas_call | solution.py:647

commit v4 on v3

--- a/solution.py
+++ b/solution.py
@@ -260,37 +260,41 @@
 
             loop(4, mix)
 
-        for a in (0, 2, 1, 3):
-
-            def partial(b):
+        order = ((0, 0), (2, 0), (0, 1), (2, 1), (1, 0), (3, 0), (1, 1), (3, 1)) if h == 0 else (
+            (2, 0), (2, 1), (3, 0), (3, 1), (0, 0), (0, 1), (1, 0), (1, 1)
+        )
+        for a, part in order:
+
+            def partial(at):
+                b = part * 2 + at
                 columns = pl.ds(pl.multiple_of((((z + a) % 4) * 4 + (y + b) % 4) * 256, 256), 256)
                 term = nn(mt[:, :512], gbuf[0, :, columns]) + nn(mt[:, 512:], gbuf[1, :, columns])
                 term = term.astype(BF16)
                 for q in range(2):
                     pb[JORDER[h * 2 + q], a * 4 + b] = term[q * 256 : (q + 1) * 256]
 
-            loop(4, partial)
+            loop(2, partial)
             if h == 0:
-                two_away(a).start()
+                two_away(a, part).start()
             elif a >= 2:
-                to_right(a).start()
+                to_right(a, part).start()
         if h == 0:
             to_left(0).start()
             to_left(1).start()
 
-    def span(a):
-        return pl.ds(a * 4, 4)
-
-    def two_away(a):
+    def span(a, part=None):
+        return pl.ds(a * 4, 4) if part is None else pl.ds(a * 4 + part * 2, 2)
+
+    def two_away(a, part=None):
         if a < 2:
-            return remote(pb.at[2, span(a)], ra.at[span(a)], out_s.at[4], p2_r.at[a], xpeer(1))
-        return remote(pb.at[2, span(a)], rb.at[span(a - 2)], out_s.at[4], p2_r.at[a], xpeer(3))
-
-    def to_right(a):
-        return remote(pb.at[1, span(a)], rl.at[span(a)], out_s.at[5], p1_r.at[a], xpeer(1))
-
-    def to_left(a):
-        return remote(pb.at[3, span(a)], rr.at[span(a)], out_s.at[6], p3_r.at[a], xpeer(3))
+            return remote(pb.at[2, span(a, part)], ra.at[span(a, part)], out_s.at[4], p2_r.at[a], xpeer(1))
+        return remote(pb.at[2, span(a, part)], rb.at[span(a - 2, part)], out_s.at[4], p2_r.at[a], xpeer(3))
+
+    def to_right(a, part=None):
+        return remote(pb.at[1, span(a, part)], rl.at[span(a, part)], out_s.at[5], p1_r.at[a], xpeer(1))
+
+    def to_left(a, part=None):
+        return remote(pb.at[3, span(a, part)], rr.at[span(a, part)], out_s.at[6], p3_r.at[a], xpeer(3))
 
     def values_half(h):
         all_values(h).wait_recv()

time: 160 us -> 159 us (level)
  no operation moved by 1% of the time
where the time goes in v4:
time: 159 us; the launch traced here: 158 us
  Pallas kernels  157 us (99%)
    pallas_call x1, Pallas kernels, local(): pl.pallas_call(kernel, out_shape=shapes, in_specs=[anywhere, vmem, vmem,...  155 us

profile of v4, /device:TPU:0, one launch (start us, length us, event | category | flops | bytes accessed | tf_op | source)
XLA Modules:
  0.0 157.9 jit_solution(11581864484289342217)
XLA Ops:
  0.6 155.4 %step.1 = (f32[2,512]{1,0:T(2,128)}, bf16[128,1024]{1,0:T(8,128)(2,1)}, f32[2,128,256]{2,1,0:T(8,128)}) custom-call(bf16[512,4096]{1,0:T(8,128)(2,1)} %grad_hbm.1, f32[2,512]{1,0:T(2,128)} %bitcast.6, s32[2,512]{1,0:T(2,128)} %bitcast.7, s32[2,512]{1,0:T(2,128)} %bitcast.8, bf16[1024,1024]{1,0:T(8,128)(2,1)} %values_hbm.1, bf16[2,4,2,128,256]{4,3,2,1,0:T(8,128)(2,1)} %bitcast.5), custom_call_target="tpu_custom_call" | custom-call | tf_op jit(solution)/shard_map/step/pallas_call | solution.py:593
  156.0 1.8 %hand_over.1 = (f32[2,512]{1,0:T(2,128)}, bf16[128,1024]{1,0:T(8,128)(2,1)}, f32[2,128,256]{2,1,0:T(8,128)}) custom-call(f32[2,512]{1,0:T(2,128)} %get-tuple-element.9.sg_in, bf16[128,1024]{1,0:T(8,128)(2,1)} %get-tuple-element.10.vg_in, f32[2,128,256]{2,1,0:T(8,128)} %get-tuple-element.11.pg_in), custom_call_target="tpu_custom_call" | custom-call | tf_op jit(solution)/shard_map/hand_over/pallas_call | solution.py:651

commit v5 on v4

--- a/solution.py
+++ b/solution.py
@@ -13,6 +13,7 @@
 JORDER = (2, 3, 1, 0)
 PLACE = (3, 2, 0, 1)
 WROW = (0, 2, 1, 3)
+GROUPS = (ORDER[:5], ORDER[5:10], ORDER[10:])
 PACKS = tuple(sum(label * 16**place for place, label in enumerate(ORDER[at : at + 5])) for at in (0, 5, 10))
 
 
@@ -362,9 +363,18 @@
             for j in (1, 3):
                 project(label, j)
 
-        def last(label):
-            relay(label).wait_recv()
-            project(label, 2)
+        def last(labels):
+            for label in labels:
+                relay(label).wait_recv()
+            place, rows = PLACE[2] * 128, pl.ds(WROW[2] * 128, 128)
+            for k in range(2):
+                total = jnp.zeros((512, 256), F32)
+                for label in labels:
+                    weights = jnp.concatenate([wg[label, 0, rows], wg[label, 1, rows]], axis=0)
+                    total = total + nt(gbuf[k, :, columns_of(label)], weights)
+                for p in range(2):
+                    here = (pl.ds(k * 512, 512), pl.ds(p * 512 + place, 128))
+                    pr[here] = pr[here] + total[:, p * 128 : (p + 1) * 128]
 
         grad_copy.wait_recv()
         for j in range(4):
@@ -373,7 +383,8 @@
         in_order(lambda label: value_copy(label, 1).start())
         in_order(pass_on)
         values_half(0)
-        in_order(last)
+        for labels in GROUPS:
+            last(labels)
 
         for k in range(2):
 

time: 159 us -> 160 us (level)
  no operation moved by 1% of the time
where the time goes in v5:
time: 160 us; the launch traced here: 158 us
  Pallas kernels  157 us (98%)
    pallas_call x1, Pallas kernels, local(): pl.pallas_call(kernel, out_shape=shapes, in_specs=[anywhere, vmem, vmem,...  155 us

profile of v5, /device:TPU:0, one launch (start us, length us, event | category | flops | bytes accessed | tf_op | source)
XLA Modules:
  0.0 157.9 jit_solution(4720985388487197880)
XLA Ops:
  0.6 155.4 %step.1 = (f32[2,512]{1,0:T(2,128)}, bf16[128,1024]{1,0:T(8,128)(2,1)}, f32[2,128,256]{2,1,0:T(8,128)}) custom-call(bf16[512,4096]{1,0:T(8,128)(2,1)} %grad_hbm.1, f32[2,512]{1,0:T(2,128)} %bitcast.6, s32[2,512]{1,0:T(2,128)} %bitcast.7, s32[2,512]{1,0:T(2,128)} %bitcast.8, bf16[1024,1024]{1,0:T(8,128)(2,1)} %values_hbm.1, bf16[2,4,2,128,256]{4,3,2,1,0:T(8,128)(2,1)} %bitcast.5), custom_call_target="tpu_custom_call" | custom-call | tf_op jit(solution)/shard_map/step/pallas_call | solution.py:604
  156.0 1.8 %hand_over.1 = (f32[2,512]{1,0:T(2,128)}, bf16[128,1024]{1,0:T(8,128)(2,1)}, f32[2,128,256]{2,1,0:T(8,128)}) custom-call(f32[2,512]{1,0:T(2,128)} %get-tuple-element.9.sg_in, bf16[128,1024]{1,0:T(8,128)(2,1)} %get-tuple-element.10.vg_in, f32[2,128,256]{2,1,0:T(8,128)} %get-tuple-element.11.pg_in), custom_call_target="tpu_custom_call" | custom-call | tf_op jit(solution)/shard_map/hand_over/pallas_call | solution.py:662
